TPU v7x, 32 devices: a whole 2x2x4 slice. The times are simulated.
32 devices in a mesh: leaf: 4 (over x, core), front: 8 (over z, y).
Axes of the slice: x: 2, y: 2, z: 4, core: 2. Of those that a mesh axis runs over, the one named last changes fastest.
Arguments:
- leaf_field: float32 [64, 128, 4, 128], P(None, ('leaf', 'front')), may hold values from -4 to 4
- leaf_source: float32 [64, 128, 4, 128], P(None, ('leaf', 'front')), may hold values from -6 to 6
- wave_squared: float32 [128, 4, 128], P(('leaf', 'front')), may hold values from 0.5 to 3
- coupling_map: int32 [32, 512], P(('leaf', 'front')), may hold values from 0 to 255
- front_rhs: float32 [64, 2048], P(None, 'front'), may hold values from -6 to 6
- row_order: int32 [2048], P('front'), may hold values from 0 to 2047, each once
- lower_panels: bfloat16 [2048, 2048], P(None, 'front'), may hold values from -0.125 to 0.125
- inverse_slots: float32 [4096, 512], P('front'), as said below
- panel_owners: int32 [4], replicated, may hold values from 0 to 7, as said below
Outputs:
- leaf_residual: float32 [64, 128, 4, 128], P(None, ('leaf', 'front'))
- solved_blocks: float32 [64, 2048], replicated
- reduced_rhs: float32 [64, 2048], P(None, 'front')
Inputs may be any that keep to these rules, and one draw needn't show every extreme that they name: `panel_owners`: 4 distinct indices of the front axis, always including 0 and 7. `inverse_slots`: each slot of 512 rows is lower triangular with diagonal entries between 0.5 and 1.5.
All inputs are finite; a program needn't handle non-finite values.
Results may differ from a plain program's by a relative error of at most 0.0019.
Values sent between devices are 32-bit elements; how exact they have to be, the bound alone decides.
No kernel may reach another device: no remote copies, remote signals or barrier semaphores. Data moves between devices by JAX's collectives and lax.ppermute only.
A program may use at most 64 MiB of HBM per device.

v0:
```python
import jax
import jax.numpy as jnp
from jax import lax
from jax.sharding import PartitionSpec as P

centre_weight = 128.0 / 30.0
face_weight = 14.0 / 30.0
cycle_weights = (0.0, 14.0 / 30.0, 3.0 / 30.0, 1.0 / 30.0)


def spread(x, axis, root):
    mine = lax.axis_index(axis) == root
    return lax.psum(jnp.where(mine, x, jnp.zeros_like(x)), axis)


def apply_operator(field, wave):
    lead = field.ndim - 3
    padded = jnp.pad(field, [(0, 0)] * lead + [(1, 1)] * 3)
    extent_x, extent_y, extent_z = field.shape[-3:]
    beside = jnp.zeros_like(field)
    for step_x in (-1, 0, 1):
        for step_y in (-1, 0, 1):
            for step_z in (-1, 0, 1):
                distance = abs(step_x) + abs(step_y) + abs(step_z)
                if distance == 0:
                    continue
                window = padded[
                    ...,
                    1 + step_x : 1 + step_x + extent_x,
                    1 + step_y : 1 + step_y + extent_y,
                    1 + step_z : 1 + step_z + extent_z,
                ]
                beside = beside + cycle_weights[distance] * window
    return (centre_weight - wave) * field - beside


def apply_inverse(block, inverse):
    return lax.dot_general(
        block,
        inverse,
        (((1,), (1,)), ((), ())),
        precision=lax.Precision.HIGHEST,
        preferred_element_type=jnp.float32,
    )


def per_device(
    leaf_field,
    leaf_source,
    wave_squared,
    coupling_map,
    front_rhs,
    row_order,
    lower_panels,
    inverse_slots,
    panel_owners,
):
    residual = leaf_source - apply_operator(leaf_field, wave_squared)
    rhs_count = residual.shape[0]
    face = residual[:, -1].reshape(rhs_count, -1)
    rows_here = front_rhs.shape[1]
    hits = (coupling_map[0][:, None] == jnp.arange(rows_here, dtype=jnp.int32)[None, :]).astype(
        jnp.float32
    )
    coupled = face_weight * jnp.dot(
        face, hits, precision=lax.Precision.HIGHEST, preferred_element_type=jnp.float32
    )
    width = inverse_slots.shape[1]
    panel_count = lower_panels.shape[0] // width
    leading = 1.0
    reduced = front_rhs + lax.psum(coupled, "leaf")
    solved_list = []
    for panel in range(panel_count):
        wanted = panel * width + jnp.arange(width, dtype=jnp.int32)
        picker = (row_order[:, None] == wanted[None, :]).astype(jnp.float32)
        partial_block = jnp.dot(
            reduced, picker, precision=lax.Precision.HIGHEST, preferred_element_type=jnp.float32
        )
        block = lax.psum(partial_block, "front")
        own_solve = apply_inverse(block, inverse_slots)
        solved = spread(own_solve, "front", panel_owners[panel])
        solved_list.append(solved)
        solved_half = solved.astype(jnp.bfloat16)
        update = jnp.dot(
            solved_half,
            lower_panels[panel * width : (panel + 1) * width],
            preferred_element_type=jnp.float32,
        )
        keep = (row_order >= (panel + 1) * width).astype(jnp.float32)
        reduced = reduced - leading * (update * keep[None, :])
    return (residual, jnp.concatenate(solved_list, axis=1), reduced)


def solution(mesh):
    return jax.shard_map(
        per_device,
        mesh=mesh,
        in_specs=(
            P(None, ("leaf", "front"), None, None),
            P(None, ("leaf", "front"), None, None),
            P(("leaf", "front"), None, None),
            P(("leaf", "front"), None),
            P(None, "front"),
            P("front"),
            P(None, "front"),
            P("front", None),
            P(),
        ),
        out_specs=(P(None, ("leaf", "front"), None, None), P(), P(None, "front")),
        check_vma=False,
    )
```

profile of v0, /device:TPU:0, one launch (start us, length us, event | category | flops | bytes accessed | tf_op | source)
XLA Modules:
  0.0 651.4 jit_solution(8520964305867727912)
XLA Ops:
  7.2 0.8 broadcast_subtract_fusion
  8.0 10.8 %fusion.56 = f32[64,4,4,128]{3,2,1,0:T(4,128)S(1)} fusion(f32[64,4,4,128]{3,2,1,0:T(4,128)} %param.10, f32[64,4,4,128]{3,2,1,0:T(4,128)} %param.9, f32[4,4,128]{2,1,0:T(4,128)S(1)} %broadcast_subtract_fusion), kind=kLoop, calls=%fused_computation.91 | loop fusion | flops 7077888 | bytes 1581056 | tf_op jit(solution)/shard_map/sub | solution.py:58
  18.9 1.0 convolution_multiply_fusion
  19.9 0.0 all-reduce.13.cloned.1.call-start
  19.9 34.3 %all-reduce.11.cloned.1.call-done = f32[64,256]{1,0:T(8,128)} async-done(((f32[64,256]{1,0:T(8,128)}), f32[64,256]{1,0:T(8,128)}) %all-reduce.11.cloned.1.call-update) | async-done | bytes 65552 | tf_op jit(solution)/shard_map/psum | solution.py:71
  54.3 0.8 add.153
  55.1 1.0 fusion.57
  56.2 0.0 all-reduce.15.cloned.1.call-start
  56.2 0.7 fusion.82
  57.5 71.1 %all-reduce.13.cloned.1.call-done = f32[64,512]{1,0:T(8,128)} async-done(((f32[64,512]{1,0:T(8,128)}), f32[64,512]{1,0:T(8,128)}) %all-reduce.13.cloned.1.call-update) | async-done | bytes 131088 | tf_op jit(solution)/shard_map/psum | solution.py:79
  128.6 2.7 convolution_select_fusion.3
  131.3 0.0 all-reduce.17.cloned.1.call-start
  131.4 70.6 %all-reduce.15.cloned.1.call-done = f32[64,512]{1,0:T(8,128)} async-done(((f32[64,512]{1,0:T(8,128)}), f32[64,512]{1,0:T(8,128)}) %all-reduce.15.cloned.1.call-update) | async-done | bytes 131088 | tf_op jit(solution)/shard_map/psum | solution.py:13
  202.0 1.1 fusion.3
  203.1 1.0 fusion.62
  204.2 0.0 all-reduce.19.cloned.1.call-start
  204.8 70.5 %all-reduce.17.cloned.1.call-done = f32[64,512]{1,0:T(8,128)} async-done(((f32[64,512]{1,0:T(8,128)}), f32[64,512]{1,0:T(8,128)}) %all-reduce.17.cloned.1.call-update) | async-done | bytes 131088 | tf_op jit(solution)/shard_map/psum | solution.py:79
  275.3 2.7 convolution_select_fusion.2
  278.0 0.0 all-reduce.21.cloned.1.call-start
  278.1 70.5 %all-reduce.19.cloned.1.call-done = f32[64,512]{1,0:T(8,128)} async-done(((f32[64,512]{1,0:T(8,128)}), f32[64,512]{1,0:T(8,128)}) %all-reduce.19.cloned.1.call-update) | async-done | bytes 131088 | tf_op jit(solution)/shard_map/psum | solution.py:13
  348.6 1.1 fusion.2
  349.6 1.0 fusion.60
  351.4 70.4 %all-reduce.21.cloned.1.call-done = f32[64,512]{1,0:T(8,128)} async-done(((f32[64,512]{1,0:T(8,128)}), f32[64,512]{1,0:T(8,128)}) %all-reduce.21.cloned.1.call-update) | async-done | bytes 131088 | tf_op jit(solution)/shard_map/psum | solution.py:79
  421.9 2.7 convolution_select_fusion.1
  424.6 70.7 %all-reduce.23.cloned.1.call-done = f32[64,512]{1,0:T(8,128)} async-done(((f32[64,512]{1,0:T(8,128)}), f32[64,512]{1,0:T(8,128)}) %all-reduce.23.cloned.1.call-update) | async-done | bytes 131088 | tf_op jit(solution)/shard_map/psum | solution.py:13
  495.3 1.1 fusion.1
  496.5 1.0 fusion.58
  498.2 70.5 %all-reduce.25.cloned.1.call-done = f32[64,512]{1,0:T(8,128)} async-done(((f32[64,512]{1,0:T(8,128)}), f32[64,512]{1,0:T(8,128)}) %all-reduce.25.cloned.1.call-update) | async-done | bytes 131088 | tf_op jit(solution)/shard_map/psum | solution.py:79
  568.7 2.7 convolution_select_fusion
  571.4 70.7 %all-reduce.27.cloned.1.call-done = f32[64,512]{1,0:T(8,128)} async-done(((f32[64,512]{1,0:T(8,128)}), f32[64,512]{1,0:T(8,128)}) %all-reduce.27.cloned.1.call-update) | async-done | bytes 131088 | tf_op jit(solution)/shard_map/psum | solution.py:13
  642.2 1.8 pad_maximum_fusion
  644.0 0.8 fusion
  (40 shorter events, 0.4 us)
Async XLA Ops:
  7.2 121.4 %copy-start = (f32[512,512]{1,0:T(8,128)S(1)}, f32[512,512]{1,0:T(8,128)}, u32[]{:S(2)}) copy-start(f32[512,512]{1,0:T(8,128)} %param.16) | copy-start | bytes 3145732
  7.2 11.7 %copy-start.10 = (s32[1,512]{1,0:T(1,128)S(1)}, s32[1,512]{1,0:T(1,128)}, u32[]{:S(2)}) copy-start(s32[1,512]{1,0:T(1,128)} %param.12) | copy-start | bytes 6148
  7.2 47.1 %all-reduce.11.cloned.1.call-start = ((), (), s32[]{:S(2)}) async-start(), calls=%async_computation | async-start | bytes 131072 | tf_op jit(solution)/shard_map/psum | solution.py:71
  8.0 46.2 %copy-start.7 = (f32[64,256]{1,0:T(8,128)S(1)}, f32[64,256]{1,0:T(8,128)}, u32[]{:S(2)}) copy-start(f32[64,256]{1,0:T(8,128)} %param.13) | copy-start | bytes 196612
  8.0 47.1 %copy-start.8 = (s32[256]{0:T(256)S(1)}, s32[256]{0:T(256)}, u32[]{:S(2)}) copy-start(s32[256]{0:T(256)} %param.14) | copy-start | bytes 3076
  8.0 48.2 %copy-start.9 = (s32[4]{0:T(128)S(1)}, s32[4]{0:T(128)}, u32[]{:S(2)}) copy-start(s32[4]{0:T(128)} %param.17) | copy-start | bytes 52
  18.8 112.5 %copy-start.2 = (f32[64,4,4,128]{3,2,1,0:T(4,128)}, f32[64,4,4,128]{3,2,1,0:T(4,128)S(1)}, u32[]{:S(2)}) copy-start(f32[64,4,4,128]{3,2,1,0:T(4,128)S(1)} %fusion.56) | copy-start | bytes 1572868
  19.9 182.2 %copy-start.1 = (bf16[2048,256]{1,0:T(8,128)(2,1)S(1)}, bf16[2048,256]{1,0:T(8,128)(2,1)}, u32[]{:S(2)}) copy-start(bf16[2048,256]{1,0:T(8,128)(2,1)} %param.15) | copy-start | bytes 3145732
  19.9 108.7 %all-reduce.13.cloned.1.call-start = ((), (), s32[]{:S(2)}) async-start(), calls=%async_computation.1 | async-start | bytes 262144 | tf_op jit(solution)/shard_map/psum | solution.py:79
  56.2 145.8 %all-reduce.15.cloned.1.call-start = ((), (), s32[]{:S(2)}) async-start(), calls=%async_computation.2 | async-start | bytes 262144 | tf_op jit(solution)/shard_map/psum | solution.py:13
  131.3 144.0 %all-reduce.17.cloned.1.call-start = ((), (), s32[]{:S(2)}) async-start(), calls=%async_computation.3 | async-start | bytes 262144 | tf_op jit(solution)/shard_map/psum | solution.py:79
  204.2 144.4 %all-reduce.19.cloned.1.call-start = ((), (), s32[]{:S(2)}) async-start(), calls=%async_computation.4 | async-start | bytes 262144 | tf_op jit(solution)/shard_map/psum | solution.py:13
  278.0 143.8 %all-reduce.21.cloned.1.call-start = ((), (), s32[]{:S(2)}) async-start(), calls=%async_computation.5 | async-start | bytes 262144 | tf_op jit(solution)/shard_map/psum | solution.py:79
  350.7 144.6 %all-reduce.23.cloned.1.call-start = ((), (), s32[]{:S(2)}) async-start(), calls=%async_computation.6 | async-start | bytes 262144 | tf_op jit(solution)/shard_map/psum | solution.py:13
  424.6 144.2 %all-reduce.25.cloned.1.call-start = ((), (), s32[]{:S(2)}) async-start(), calls=%async_computation.7 | async-start | bytes 262144 | tf_op jit(solution)/shard_map/psum | solution.py:79
  495.3 146.9 %copy-start.3 = (f32[64,512]{1,0:T(8,128)S(1)}, f32[64,512]{1,0:T(8,128)}, u32[]{:S(2)}) copy-start(f32[64,512]{1,0:T(8,128)} %all-reduce.15.cloned.1.call-done) | copy-start | bytes 393220
  495.3 146.9 %copy-start.4 = (f32[64,512]{1,0:T(8,128)S(1)}, f32[64,512]{1,0:T(8,128)}, u32[]{:S(2)}) copy-start(f32[64,512]{1,0:T(8,128)} %all-reduce.19.cloned.1.call-done) | copy-start | bytes 393220
  495.3 146.9 %copy-start.5 = (f32[64,512]{1,0:T(8,128)S(1)}, f32[64,512]{1,0:T(8,128)}, u32[]{:S(2)}) copy-start(f32[64,512]{1,0:T(8,128)} %all-reduce.23.cloned.1.call-done) | copy-start | bytes 393220
  497.5 144.7 %all-reduce.27.cloned.1.call-start = ((), (), s32[]{:S(2)}) async-start(), calls=%async_computation.8 | async-start | bytes 262144 | tf_op jit(solution)/shard_map/psum | solution.py:13
  642.2 1.8 copy-start.6
Sparse Core Ops, SparseCore 0:
  20.0 34.1 all-reduce.10
  58.2 70.3 all-reduce.12
  132.5 69.4 all-reduce.14
  205.8 69.4 all-reduce.16
  279.1 69.4 all-reduce.18
  352.3 69.4 all-reduce.20
  425.8 69.4 all-reduce.22
  499.2 69.4 all-reduce.24
  572.7 69.4 all-reduce.26
where the time goes:
time: 652 us; the launch traced here: 651 us
  waiting for transfers between devices  600 us (92%)
  matrix products  20 us (3%)
  between operations  16.5 us (3%)
  other arithmetic  14.2 us (2%)
    psum x4, waiting for transfers between devices, spread(): return lax.psum(jnp.where(mine, x, jnp.zeros_like(x)), axis)  283 us
    psum x4, waiting for transfers between devices, per_device(): block = lax.psum(partial_block, 'front')  283 us
    psum x1, waiting for transfers between devices, per_device(): reduced = front_rhs + lax.psum(coupled, 'leaf')  34.3 us
  transfers between devices with their start and end apart: 9, of which 9 were waited for; matrix products, arithmetic and copies ran while one was open for 0% of the time, Pallas kernels for 0%

commit v1 on v0

v1 whole, which is shorter than its diff:
```python
import functools

import jax
import jax.numpy as jnp
from jax import lax
from jax.experimental import pallas as pl
from jax.experimental.pallas import tpu as pltpu
from jax.sharding import PartitionSpec as P

centre_weight = 128.0 / 30.0
face_weight = 14.0 / 30.0
edge_weight = 3.0 / 30.0
corner_weight = 1.0 / 30.0

VMEM = pl.BlockSpec(memory_space=pltpu.VMEM)
SMEM = pl.BlockSpec(memory_space=pltpu.SMEM)
F32 = jnp.float32
BF16 = jnp.bfloat16


def params():
    return pltpu.CompilerParams(vmem_limit_bytes=16 << 20)


def cost(flops, moved):
    return pl.CostEstimate(flops=flops, bytes_accessed=moved, transcendentals=0)


def dot_nt(a, b):
    return lax.dot_general(a, b, (((1,), (1,)), ((), ())), preferred_element_type=F32)


def split3(x):
    high = x.astype(BF16)
    rest = x - high.astype(F32)
    middle = rest.astype(BF16)
    low = (rest - middle.astype(F32)).astype(BF16)
    return high, middle, low


def select_columns(x, chosen):
    count = x.shape[0]
    parts = dot_nt(jnp.concatenate(split3(x), axis=0), chosen)
    return (parts[2 * count :] + parts[count : 2 * count]) + parts[:count]


def rows_of(index, size, total):
    return pl.ds(pl.multiple_of((index & (total // size - 1)) * size, 8), size)


def leaf_kernel(gx, gy, lanes, blocks, field, source, wave, cmap, residual, *rest):
    chunks, face, coupled = rest[:lanes], rest[lanes], rest[lanes + 1]
    step = pl.program_id(0)
    rows = field.shape[0]
    cells = gx * gy
    here = rows // cells
    width = field.shape[1]
    v = field[...]
    row = lax.broadcasted_iota(jnp.int32, (rows, width), 0) % cells
    lane = lax.broadcasted_iota(jnp.int32, (rows, width), 1)
    zero = jnp.zeros_like(v)
    left = jnp.where(lane > 0, pltpu.roll(v, 1, 1), zero)
    right = jnp.where(lane < width - 1, pltpu.roll(v, width - 1, 1), zero)
    sides = left + right
    once = face_weight * v + edge_weight * sides
    twice = edge_weight * v + corner_weight * sides
    y = row % gy

    def shift_y(p):
        below = jnp.where(y > 0, pltpu.roll(p, 1, 0), zero)
        above = jnp.where(y < gy - 1, pltpu.roll(p, rows - 1, 0), zero)
        return below + above

    around = once + shift_y(twice)
    below = jnp.where(row >= gy, pltpu.roll(around, gy, 0), zero)
    above = jnp.where(row < cells - gy, pltpu.roll(around, rows - gy, 0), zero)
    beside = face_weight * sides + shift_y(once) + (below + above)
    weight = centre_weight - wave[...]
    centre = (v.reshape(here, cells, width) * weight[None]).reshape(rows, width)
    residual[...] = source[...] - (centre - beside)
    for j in range(gy):
        face[pl.ds(step * here, here), j * width : (j + 1) * width] = residual[
            pl.ds(cells - gy + j, here, stride=cells), :
        ]

    @pl.when(step == blocks - 1)
    def _():
        slots = coupled.shape[1]
        hits = lax.broadcasted_iota(jnp.int32, (slots, cmap.shape[1]), 0) == cmap[...]
        coupled[...] = face_weight * select_columns(face[...], hits.astype(BF16))
        me = lax.axis_index("leaf")
        size = chunks[0].shape[0]
        for m in range(lanes):
            chunks[m][...] = coupled[rows_of(me ^ m, size, coupled.shape[0]), :]


def picker(order, panel, width):
    rows = order.shape[1]
    wanted = lax.broadcasted_iota(jnp.int32, (width, rows), 0) + panel * width
    return (wanted == order).astype(BF16)


def first_kernel(lanes, width, *refs):
    chunks, front, order, reduced, partial = refs[:lanes], *refs[lanes:]
    size = chunks[0].shape[0]
    total = front[rows_of(lax.axis_index("leaf"), size, front.shape[0]), :]
    for chunk in chunks:
        total = total + chunk[...]
    reduced[...] = total
    partial[...] = select_columns(total, picker(order[...], 0, width))


def split_kernel(inverse, high, middle, low):
    high[...], middle[...], low[...] = split3(inverse[...])


def solve_kernel(panel, a, b, high, middle, low, owners, out):
    block = a[...] + b[...]
    count = block.shape[0]
    bh, bm, bl = split3(block)
    first = dot_nt(jnp.concatenate([bh, bm, bl], axis=0), high[...])
    second = dot_nt(jnp.concatenate([bh, bm], axis=0), middle[...])
    third = dot_nt(bh, low[...])
    small = third + second[count:] + first[2 * count :]
    solved = (small + (second[:count] + first[count : 2 * count])) + first[:count]
    mine = owners[panel] == lax.axis_index("front")
    out[...] = jnp.where(mine, solved, jnp.zeros_like(solved))


def update_kernel(panel, last, a, b, lower, order, reduced_in, solved, reduced, *partial):
    width = a.shape[1]
    block = a[...] + b[...]
    solved[...] = block
    update = jnp.dot(block.astype(BF16), lower[...], preferred_element_type=F32)
    keep = order[...] >= (panel + 1) * width
    left = reduced_in[...] - jnp.where(keep, update, jnp.zeros_like(update))
    reduced[...] = left
    if not last:
        partial[0][...] = select_columns(left, picker(order[...], panel + 1, width))


def gather_kernel(groups, panels, *refs):
    solved_in, reduced_in = refs[: panels * groups], refs[panels * groups : (panels + 1) * groups]
    solved, reduced = refs[(panels + 1) * groups :]
    me = lax.axis_index("leaf")
    size, width = solved_in[0].shape
    for m in range(groups):
        rows = rows_of(me ^ m, size, solved.shape[0])
        reduced[rows, :] = reduced_in[m][...]
        for panel in range(panels):
            solved[rows, panel * width : (panel + 1) * width] = solved_in[panel * groups + m][...]


def per_device(
    lanes,
    fronts,
    leaf_field,
    leaf_source,
    wave_squared,
    coupling_map,
    front_rhs,
    row_order,
    lower_panels,
    inverse_slots,
    panel_owners,
):
    rhs_count, gx, gy, gz = leaf_field.shape
    cells = gx * gy
    rows_here = front_rhs.shape[1]
    width = inverse_slots.shape[1]
    panels = lower_panels.shape[0] // width
    groups = min(lanes, rhs_count // 8)
    share = rhs_count // groups

    def trade(x, axis, count, mask):
        return lax.ppermute(x, axis, [(i, i ^ mask) for i in range(count)])

    def butterfly(x):
        mask = 1
        while mask * 2 < fronts:
            if mask * 4 < fronts:
                r = [trade(x, "front", fronts, mask * k) for k in (3, 2, 1)]
                x = (x + r[2]) + (r[1] + r[0])
                mask *= 4
            else:
                x = x + trade(x, "front", fronts, mask)
                mask *= 2
        return x, trade(x, "front", fronts, mask)

    blocks = 4
    rows = rhs_count * cells
    field = leaf_field.reshape(rows, gz)
    source = leaf_source.reshape(rows, gz)
    wave = wave_squared.reshape(cells, gz)
    order = row_order.reshape(1, rows_here)
    piece = jax.ShapeDtypeStruct((share, rows_here), F32)
    tile = pl.BlockSpec((rows // blocks, gz), lambda i: (i, 0))
    whole = lambda shape: pl.BlockSpec(shape, lambda i: (0,) * len(shape))
    residual, *chunks = pl.pallas_call(
        functools.partial(leaf_kernel, gx, gy, lanes, blocks),
        grid=(blocks,),
        in_specs=[tile, tile, whole(wave.shape), whole(coupling_map.shape)],
        out_specs=[tile] + [whole(piece.shape)] * lanes,
        out_shape=[jax.ShapeDtypeStruct((rows, gz), F32)] + [piece] * lanes,
        scratch_shapes=[
            pltpu.VMEM((rhs_count, gy * gz), F32),
            pltpu.VMEM((rhs_count, rows_here), F32),
        ],
        compiler_params=params(),
        cost_estimate=cost(40 * rows * gz, 12 * rows * gz),
        name="leaf",
    )(field, source, wave, coupling_map)
    chunks = [chunks[0]] + [trade(chunks[m], "leaf", lanes, m) for m in range(1, lanes)]
    block_shape = jax.ShapeDtypeStruct((share, width), F32)
    reduced, partial = pl.pallas_call(
        functools.partial(first_kernel, lanes, width),
        in_specs=[VMEM] * (lanes + 2),
        out_specs=[VMEM, VMEM],
        out_shape=[piece, block_shape],
        compiler_params=params(),
        name="first",
    )(*chunks, front_rhs, order)
    pieces = pl.pallas_call(
        split_kernel,
        in_specs=[VMEM],
        out_specs=[VMEM] * 3,
        out_shape=[jax.ShapeDtypeStruct(inverse_slots.shape, BF16)] * 3,
        compiler_params=params(),
        name="split",
    )(inverse_slots)
    solved_list = []
    for panel in range(panels):
        last = panel == panels - 1
        a, b = butterfly(partial)
        own = pl.pallas_call(
            functools.partial(solve_kernel, panel),
            in_specs=[VMEM] * 5 + [SMEM],
            out_specs=VMEM,
            out_shape=block_shape,
            compiler_params=params(),
            name="solve",
        )(a, b, *pieces, panel_owners)
        a, b = butterfly(own)
        outs = pl.pallas_call(
            functools.partial(update_kernel, panel, last),
            in_specs=[VMEM] * 5,
            out_specs=[VMEM] * (2 if last else 3),
            out_shape=[block_shape, piece] + ([] if last else [block_shape]),
            compiler_params=params(),
            name="update",
        )(a, b, lower_panels[panel * width : (panel + 1) * width], order, reduced)
        solved, reduced = outs[:2]
        if not last:
            partial = outs[2]
        solved_list.append(solved)
    gathered = []
    for x in solved_list + [reduced]:
        gathered += [x] + [trade(x, "leaf", lanes, m) for m in range(1, groups)]
    solved, reduced = pl.pallas_call(
        functools.partial(gather_kernel, groups, panels),
        in_specs=[VMEM] * len(gathered),
        out_specs=[VMEM, VMEM],
        out_shape=[
            jax.ShapeDtypeStruct((rhs_count, panels * width), F32),
            jax.ShapeDtypeStruct((rhs_count, rows_here), F32),
        ],
        compiler_params=params(),
        name="collect",
    )(*gathered)
    return (residual.reshape(leaf_field.shape), solved, reduced)


def solution(mesh):
    return jax.shard_map(
        functools.partial(per_device, mesh.shape["leaf"], mesh.shape["front"]),
        mesh=mesh,
        in_specs=(
            P(None, ("leaf", "front"), None, None),
            P(None, ("leaf", "front"), None, None),
            P(("leaf", "front"), None, None),
            P(("leaf", "front"), None),
            P(None, "front"),
            P("front"),
            P(None, "front"),
            P("front", None),
            P(),
        ),
        out_specs=(P(None, ("leaf", "front"), None, None), P(), P(None, "front")),
        check_vma=False,
    )
```

time: 652 us -> 121 us (0.19)
  waiting for transfers between devices: 600 us -> 43 us
  starting transfers between devices: 0.37 us -> 61.7 us
  matrix products: 20 us -> 0 us
  between operations: 16.5 us -> 0.75 us
  other arithmetic: 14.2 us -> 0.09 us
  Pallas kernels: 0 us -> 8.97 us
    psum x9 -> x0, waiting for transfers between devices: 599 us -> none  [the longest x4 283 us: spread(): return lax.psum(jnp.where(mine, x, jnp.zeros_like(x)), axis)]
    ppermute x0 -> x50, starting transfers between devices: none -> 61.7 us  [trade(): return lax.ppermute(x, axis, [(i, i ^ mask) for i in range(count)])]
    ppermute x0 -> x50, waiting for transfers between devices: none -> 43 us  [trade(): return lax.ppermute(x, axis, [(i, i ^ mask) for i in range(count)])]
    dot_general x13 -> x0, matrix products: 20 us -> none  [the longest x4 10.7 us: apply_inverse(): lax.dot_general(block, inverse, (((1,), (1,)), ((), ())), precision=lax.P...]
    sub x2 -> x0, other arithmetic: 11.6 us -> none  [the longest x1 10.8 us: per_device(): residual = leaf_source - apply_operator(leaf_field, wave_squared)]
    pallas_call x0 -> x12, Pallas kernels: none -> 8.97 us  [the longest x4 4.29 us: per_device(): pl.pallas_call(functools.partial(solve_kernel, panel), in_specs=[VMEM] *...]
  transfers between devices with their start and end apart: 9 -> 50, of which waited for: 9 -> 34; matrix products, arithmetic and copies ran while one was open for 0% -> 0% of each run, Pallas kernels for 0% -> 0%
where the time goes in v1:
time: 121 us; the launch traced here: 120 us
  starting transfers between devices  61.7 us (51%)
  waiting for transfers between devices  43 us (36%)
  Pallas kernels  8.97 us (7%)
  local copies, waits for them, and re-layouts  5.79 us (5%)
    ppermute x50, starting transfers between devices, trade(): return lax.ppermute(x, axis, [(i, i ^ mask) for i in range(count)])  61.7 us
    ppermute x50, waiting for transfers between devices, trade(): return lax.ppermute(x, axis, [(i, i ^ mask) for i in range(count)])  43 us
    unnamed x18, local copies, waits for them, and re-layouts  5.72 us
    pallas_call x4, Pallas kernels, per_device(): pl.pallas_call(functools.partial(solve_kernel, panel), in_specs=[VMEM] *...  4.29 us
  transfers between devices with their start and end apart: 50, of which 34 were waited for; matrix products, arithmetic and copies ran while one was open for 0% of the time, Pallas kernels for 0%

profile of v1, /device:TPU:0, one launch (start us, length us, event | category | flops | bytes accessed | tf_op | source)
XLA Modules:
  0.0 120.4 jit_solution(9788239797186872129)
XLA Ops:
  4.2 2.4 %leaf.1 = (f32[1024,128]{1,0:T(8,128)}, f32[16,256]{1,0:T(8,128)S(1)}, f32[16,256]{1,0:T(8,128)S(1)}, f32[16,256]{1,0:T(8,128)S(1)}, f32[16,256]{1,0:T(8,128)S(1)}) custom-call(f32[1024,128]{1,0:T(8,128)S(1)} %bitcast.5, f32[1024,128]{1,0:T(8,128)S(1)} %bitcast.6, f32[16,128]{1,0:T(8,128)S(1)} %bitcast.12, s32[1,512]{1,0:T(1,128)S(1)} %copy-done.7), custom_call_target="tpu_custom_call" | custom-call | flops 5242880 | bytes 1572864 | tf_op jit(solution)/shard_map/leaf/pallas_call | solution.py:199
  7.1 2.5 %collective-permute-start.1 = (f32[16,256]{1,0:T(8,128)S(1)}, f32[16,256]{1,0:T(8,128)S(1)}, u32[]{:S(2)}, u32[]{:S(2)}) collective-permute-start(f32[16,256]{1,0:T(8,128)S(1)} %get-tuple-element.29), channel_id=1, source_target_pairs={{0,16},{8,24},{16,0},{24,8},{1,17},{9,25},{17,1},{25,9},{2,18},{10... | collective-permute-start | bytes 49160 | tf_op jit(solution)/shard_map/ppermute | solution.py:176
  9.7 1.6 %collective-permute-done.1.refs_2_ = f32[16,256]{1,0:T(8,128)S(1)} collective-permute-done((f32[16,256]{1,0:T(8,128)S(1)}, f32[16,256]{1,0:T(8,128)S(1)}, u32[]{:S(2)}, u32[]{:S(2)}) %collective-permute-start.1) | collective-permute-done | bytes 16416 | tf_op jit(solution)/shard_map/ppermute | solution.py:176
  14.5 2.6 %collective-permute-start.5 = (f32[16,512]{1,0:T(8,128)S(1)}, f32[16,512]{1,0:T(8,128)S(1)}, u32[]{:S(2)}, u32[]{:S(2)}) collective-permute-start(f32[16,512]{1,0:T(8,128)S(1)} %get-tuple-element.31), channel_id=1, source_target_pairs={{0,3},{1,2},{2,1},{3,0},{4,7},{5,6},{6,5},{7,4},{8,11},{9,10},{10,... | collective-permute-start | bytes 98312 | tf_op jit(solution)/shard_map/ppermute | solution.py:176
  19.3 1.6 %collective-permute-done.4 = f32[16,512]{1,0:T(8,128)S(1)} collective-permute-done((f32[16,512]{1,0:T(8,128)S(1)}, f32[16,512]{1,0:T(8,128)S(1)}, u32[]{:S(2)}, u32[]{:S(2)}) %collective-permute-start.4) | collective-permute-done | bytes 32800 | tf_op jit(solution)/shard_map/ppermute | solution.py:176
  21.4 2.7 %collective-permute-start.6 = (f32[16,512]{1,0:T(8,128)S(1)}, f32[16,512]{1,0:T(8,128)S(1)}, u32[]{:S(2)}, u32[]{:S(2)}) collective-permute-start(f32[16,512]{1,0:T(8,128)S(1)} %add_add_fusion.7.a), channel_id=1, source_target_pairs={{0,4},{1,5},{2,6},{3,7},{4,0},{5,1},{6,2},{7,3},{8,12},{9,13},{10,... | collective-permute-start | bytes 98312 | tf_op jit(solution)/shard_map/ppermute | solution.py:176
  24.3 2.0 %collective-permute-done.6.b = f32[16,512]{1,0:T(8,128)S(1)} collective-permute-done((f32[16,512]{1,0:T(8,128)S(1)}, f32[16,512]{1,0:T(8,128)S(1)}, u32[]{:S(2)}, u32[]{:S(2)}) %collective-permute-start.6) | collective-permute-done | bytes 32800 | tf_op jit(solution)/shard_map/ppermute | solution.py:176
  33.9 2.7 %collective-permute-start.10 = (f32[16,512]{1,0:T(8,128)S(1)}, f32[16,512]{1,0:T(8,128)S(1)}, u32[]{:S(2)}, u32[]{:S(2)}) collective-permute-start(f32[16,512]{1,0:T(8,128)S(1)} %add_add_fusion.6.a), channel_id=1, source_target_pairs={{0,4},{1,5},{2,6},{3,7},{4,0},{5,1},{6,2},{7,3},{8,12},{9,13},{10,... | collective-permute-start | bytes 98312 | tf_op jit(solution)/shard_map/ppermute | solution.py:176
  36.7 2.2 %collective-permute-done.10.b = f32[16,512]{1,0:T(8,128)S(1)} collective-permute-done((f32[16,512]{1,0:T(8,128)S(1)}, f32[16,512]{1,0:T(8,128)S(1)}, u32[]{:S(2)}, u32[]{:S(2)}) %collective-permute-start.10) | collective-permute-done | bytes 32800 | tf_op jit(solution)/shard_map/ppermute | solution.py:176
  39.1 2.5 %collective-permute-start.16 = (f32[16,512]{1,0:T(8,128)S(1)}, f32[16,512]{1,0:T(8,128)S(1)}, u32[]{:S(2)}, u32[]{:S(2)}) collective-permute-start(f32[16,512]{1,0:T(8,128)S(1)} %get-tuple-element.37), channel_id=1, source_target_pairs={{0,3},{1,2},{2,1},{3,0},{4,7},{5,6},{6,5},{7,4},{8,11},{9,10},{10,... | collective-permute-start | bytes 98312 | tf_op jit(solution)/shard_map/ppermute | solution.py:176
  43.9 1.6 %collective-permute-done.15 = f32[16,512]{1,0:T(8,128)S(1)} collective-permute-done((f32[16,512]{1,0:T(8,128)S(1)}, f32[16,512]{1,0:T(8,128)S(1)}, u32[]{:S(2)}, u32[]{:S(2)}) %collective-permute-start.15) | collective-permute-done | bytes 32800 | tf_op jit(solution)/shard_map/ppermute | solution.py:176
  46.0 2.6 %collective-permute-start.17 = (f32[16,512]{1,0:T(8,128)S(1)}, f32[16,512]{1,0:T(8,128)S(1)}, u32[]{:S(2)}, u32[]{:S(2)}) collective-permute-start(f32[16,512]{1,0:T(8,128)S(1)} %add_add_fusion.5.a), channel_id=1, source_target_pairs={{0,4},{1,5},{2,6},{3,7},{4,0},{5,1},{6,2},{7,3},{8,12},{9,13},{10,... | collective-permute-start | bytes 98312 | tf_op jit(solution)/shard_map/ppermute | solution.py:176
  48.7 2.2 %collective-permute-done.17.b = f32[16,512]{1,0:T(8,128)S(1)} collective-permute-done((f32[16,512]{1,0:T(8,128)S(1)}, f32[16,512]{1,0:T(8,128)S(1)}, u32[]{:S(2)}, u32[]{:S(2)}) %collective-permute-start.17) | collective-permute-done | bytes 32800 | tf_op jit(solution)/shard_map/ppermute | solution.py:176
  52.0 1.6 %collective-permute-start.20 = (f32[16,512]{1,0:T(8,128)S(1)}, f32[16,512]{1,0:T(8,128)S(1)}, u32[]{:S(2)}, u32[]{:S(2)}) collective-permute-start(f32[16,512]{1,0:T(8,128)S(1)} %solve.5), channel_id=1, source_target_pairs={{0,3},{1,2},{2,1},{3,0},{4,7},{5,6},{6,5},{7,4},{8,11},{9,10},{10,... | collective-permute-start | bytes 98312 | tf_op jit(solution)/shard_map/ppermute | solution.py:176
  57.9 2.7 %collective-permute-start.21 = (f32[16,512]{1,0:T(8,128)S(1)}, f32[16,512]{1,0:T(8,128)S(1)}, u32[]{:S(2)}, u32[]{:S(2)}) collective-permute-start(f32[16,512]{1,0:T(8,128)S(1)} %add_add_fusion.4.a), channel_id=1, source_target_pairs={{0,4},{1,5},{2,6},{3,7},{4,0},{5,1},{6,2},{7,3},{8,12},{9,13},{10,... | collective-permute-start | bytes 98312 | tf_op jit(solution)/shard_map/ppermute | solution.py:176
  60.5 2.2 %collective-permute-done.21.b = f32[16,512]{1,0:T(8,128)S(1)} collective-permute-done((f32[16,512]{1,0:T(8,128)S(1)}, f32[16,512]{1,0:T(8,128)S(1)}, u32[]{:S(2)}, u32[]{:S(2)}) %collective-permute-start.21) | collective-permute-done | bytes 32800 | tf_op jit(solution)/shard_map/ppermute | solution.py:176
  63.0 2.5 %collective-permute-start.27 = (f32[16,512]{1,0:T(8,128)S(1)}, f32[16,512]{1,0:T(8,128)S(1)}, u32[]{:S(2)}, u32[]{:S(2)}) collective-permute-start(f32[16,512]{1,0:T(8,128)S(1)} %get-tuple-element.40), channel_id=1, source_target_pairs={{0,3},{1,2},{2,1},{3,0},{4,7},{5,6},{6,5},{7,4},{8,11},{9,10},{10,... | collective-permute-start | bytes 98312 | tf_op jit(solution)/shard_map/ppermute | solution.py:176
  70.0 2.6 %collective-permute-start.28 = (f32[16,512]{1,0:T(8,128)S(1)}, f32[16,512]{1,0:T(8,128)S(1)}, u32[]{:S(2)}, u32[]{:S(2)}) collective-permute-start(f32[16,512]{1,0:T(8,128)S(1)} %add_add_fusion.3.a), channel_id=1, source_target_pairs={{0,4},{1,5},{2,6},{3,7},{4,0},{5,1},{6,2},{7,3},{8,12},{9,13},{10,... | collective-permute-start | bytes 98312 | tf_op jit(solution)/shard_map/ppermute | solution.py:176
  72.6 2.3 %collective-permute-done.28.b = f32[16,512]{1,0:T(8,128)S(1)} collective-permute-done((f32[16,512]{1,0:T(8,128)S(1)}, f32[16,512]{1,0:T(8,128)S(1)}, u32[]{:S(2)}, u32[]{:S(2)}) %collective-permute-start.28) | collective-permute-done | bytes 32800 | tf_op jit(solution)/shard_map/ppermute | solution.py:176
  76.0 1.6 %collective-permute-start.31 = (f32[16,512]{1,0:T(8,128)S(1)}, f32[16,512]{1,0:T(8,128)S(1)}, u32[]{:S(2)}, u32[]{:S(2)}) collective-permute-start(f32[16,512]{1,0:T(8,128)S(1)} %solve.6), channel_id=1, source_target_pairs={{0,3},{1,2},{2,1},{3,0},{4,7},{5,6},{6,5},{7,4},{8,11},{9,10},{10,... | collective-permute-start | bytes 98312 | tf_op jit(solution)/shard_map/ppermute | solution.py:176
  77.9 1.6 %collective-permute-start.29 = (f32[16,512]{1,0:T(8,128)S(1)}, f32[16,512]{1,0:T(8,128)S(1)}, u32[]{:S(2)}, u32[]{:S(2)}) collective-permute-start(f32[16,512]{1,0:T(8,128)S(1)} %solve.6), channel_id=1, source_target_pairs={{0,1},{1,0},{2,3},{3,2},{4,5},{5,4},{6,7},{7,6},{8,9},{9,8},{10,11... | collective-permute-start | bytes 98312 | tf_op jit(solution)/shard_map/ppermute | solution.py:176
  79.5 1.7 %collective-permute-done.31 = f32[16,512]{1,0:T(8,128)S(1)} collective-permute-done((f32[16,512]{1,0:T(8,128)S(1)}, f32[16,512]{1,0:T(8,128)S(1)}, u32[]{:S(2)}, u32[]{:S(2)}) %collective-permute-start.31) | collective-permute-done | bytes 32800 | tf_op jit(solution)/shard_map/ppermute | solution.py:176
  81.8 2.8 %collective-permute-start.32 = (f32[16,512]{1,0:T(8,128)S(1)}, f32[16,512]{1,0:T(8,128)S(1)}, u32[]{:S(2)}, u32[]{:S(2)}) collective-permute-start(f32[16,512]{1,0:T(8,128)S(1)} %add_add_fusion.2.a), channel_id=1, source_target_pairs={{0,4},{1,5},{2,6},{3,7},{4,0},{5,1},{6,2},{7,3},{8,12},{9,13},{10,... | collective-permute-start | bytes 98312 | tf_op jit(solution)/shard_map/ppermute | solution.py:176
  84.6 2.1 %collective-permute-done.32.b = f32[16,512]{1,0:T(8,128)S(1)} collective-permute-done((f32[16,512]{1,0:T(8,128)S(1)}, f32[16,512]{1,0:T(8,128)S(1)}, u32[]{:S(2)}, u32[]{:S(2)}) %collective-permute-start.32) | collective-permute-done | bytes 32800 | tf_op jit(solution)/shard_map/ppermute | solution.py:176
  87.0 2.9 %collective-permute-start.38 = (f32[16,512]{1,0:T(8,128)S(1)}, f32[16,512]{1,0:T(8,128)S(1)}, u32[]{:S(2)}, u32[]{:S(2)}) collective-permute-start(f32[16,512]{1,0:T(8,128)S(1)} %get-tuple-element.43), channel_id=1, source_target_pairs={{0,3},{1,2},{2,1},{3,0},{4,7},{5,6},{6,5},{7,4},{8,11},{9,10},{10,... | collective-permute-start | bytes 98312 | tf_op jit(solution)/shard_map/ppermute | solution.py:176
  91.8 2.0 %collective-permute-done.37 = f32[16,512]{1,0:T(8,128)S(1)} collective-permute-done((f32[16,512]{1,0:T(8,128)S(1)}, f32[16,512]{1,0:T(8,128)S(1)}, u32[]{:S(2)}, u32[]{:S(2)}) %collective-permute-start.37) | collective-permute-done | bytes 32800 | tf_op jit(solution)/shard_map/ppermute | solution.py:176
  94.0 3.0 %collective-permute-start.39 = (f32[16,512]{1,0:T(8,128)S(1)}, f32[16,512]{1,0:T(8,128)S(1)}, u32[]{:S(2)}, u32[]{:S(2)}) collective-permute-start(f32[16,512]{1,0:T(8,128)S(1)} %add_add_fusion.1.a), channel_id=1, source_target_pairs={{0,4},{1,5},{2,6},{3,7},{4,0},{5,1},{6,2},{7,3},{8,12},{9,13},{10,... | collective-permute-start | bytes 98312 | tf_op jit(solution)/shard_map/ppermute | solution.py:176
  96.9 1.9 %collective-permute-done.39.b = f32[16,512]{1,0:T(8,128)S(1)} collective-permute-done((f32[16,512]{1,0:T(8,128)S(1)}, f32[16,512]{1,0:T(8,128)S(1)}, u32[]{:S(2)}, u32[]{:S(2)}) %collective-permute-start.39) | collective-permute-done | bytes 32800 | tf_op jit(solution)/shard_map/ppermute | solution.py:176
  99.9 1.9 %collective-permute-start.42 = (f32[16,512]{1,0:T(8,128)S(1)}, f32[16,512]{1,0:T(8,128)S(1)}, u32[]{:S(2)}, u32[]{:S(2)}) collective-permute-start(f32[16,512]{1,0:T(8,128)S(1)} %solve.7), channel_id=1, source_target_pairs={{0,3},{1,2},{2,1},{3,0},{4,7},{5,6},{6,5},{7,4},{8,11},{9,10},{10,... | collective-permute-start | bytes 98312 | tf_op jit(solution)/shard_map/ppermute | solution.py:176
  101.9 1.6 %collective-permute-start.40 = (f32[16,512]{1,0:T(8,128)S(1)}, f32[16,512]{1,0:T(8,128)S(1)}, u32[]{:S(2)}, u32[]{:S(2)}) collective-permute-start(f32[16,512]{1,0:T(8,128)S(1)} %solve.7), channel_id=1, source_target_pairs={{0,1},{1,0},{2,3},{3,2},{4,5},{5,4},{6,7},{7,6},{8,9},{9,8},{10,11... | collective-permute-start | bytes 98312 | tf_op jit(solution)/shard_map/ppermute | solution.py:176
  105.8 2.9 %collective-permute-start.43 = (f32[16,512]{1,0:T(8,128)S(1)}, f32[16,512]{1,0:T(8,128)S(1)}, u32[]{:S(2)}, u32[]{:S(2)}) collective-permute-start(f32[16,512]{1,0:T(8,128)S(1)} %add_add_fusion.a), channel_id=1, source_target_pairs={{0,4},{1,5},{2,6},{3,7},{4,0},{5,1},{6,2},{7,3},{8,12},{9,13},{10,... | collective-permute-start | bytes 98312 | tf_op jit(solution)/shard_map/ppermute | solution.py:176
  116.6 2.9 %collective-permute-done.48.refs_18_ = f32[16,256]{1,0:T(8,128)S(1)} collective-permute-done((f32[16,256]{1,0:T(8,128)S(1)}, f32[16,256]{1,0:T(8,128)S(1)}, u32[]{:S(2)}, u32[]{:S(2)}) %collective-permute-start.48) | collective-permute-done | bytes 16416 | tf_op jit(solution)/shard_map/ppermute | solution.py:176
  (107 shorter events, 47.8 us)
Async XLA Ops:
  7.1 4.2 %collective-permute-start.1 = (f32[16,256]{1,0:T(8,128)S(1)}, f32[16,256]{1,0:T(8,128)S(1)}, u32[]{:S(2)}, u32[]{:S(2)}) collective-permute-start(f32[16,256]{1,0:T(8,128)S(1)} %get-tuple-element.29), channel_id=1, source_target_pairs={{0,16},{8,24},{16,0},{24,8},{1,17},{9,25},{17,1},{25,9},{2,18},{10... | collective-permute-start | bytes 49160 | tf_op jit(solution)/shard_map/ppermute | solution.py:176
  14.5 4.8 %collective-permute-start.5 = (f32[16,512]{1,0:T(8,128)S(1)}, f32[16,512]{1,0:T(8,128)S(1)}, u32[]{:S(2)}, u32[]{:S(2)}) collective-permute-start(f32[16,512]{1,0:T(8,128)S(1)} %get-tuple-element.31), channel_id=1, source_target_pairs={{0,3},{1,2},{2,1},{3,0},{4,7},{5,6},{6,5},{7,4},{8,11},{9,10},{10,... | collective-permute-start | bytes 98312 | tf_op jit(solution)/shard_map/ppermute | solution.py:176
  17.0 3.9 %collective-permute-start.4 = (f32[16,512]{1,0:T(8,128)S(1)}, f32[16,512]{1,0:T(8,128)S(1)}, u32[]{:S(2)}, u32[]{:S(2)}) collective-permute-start(f32[16,512]{1,0:T(8,128)S(1)} %get-tuple-element.31), channel_id=1, source_target_pairs={{0,2},{1,3},{2,0},{3,1},{4,6},{5,7},{6,4},{7,5},{8,10},{9,11},{10,... | collective-permute-start | bytes 98312 | tf_op jit(solution)/shard_map/ppermute | solution.py:176
  17.5 3.9 %collective-permute-start.3 = (f32[16,512]{1,0:T(8,128)S(1)}, f32[16,512]{1,0:T(8,128)S(1)}, u32[]{:S(2)}, u32[]{:S(2)}) collective-permute-start(f32[16,512]{1,0:T(8,128)S(1)} %get-tuple-element.31), channel_id=1, source_target_pairs={{0,1},{1,0},{2,3},{3,2},{4,5},{5,4},{6,7},{7,6},{8,9},{9,8},{10,11... | collective-permute-start | bytes 98312 | tf_op jit(solution)/shard_map/ppermute | solution.py:176
  21.4 4.9 %collective-permute-start.6 = (f32[16,512]{1,0:T(8,128)S(1)}, f32[16,512]{1,0:T(8,128)S(1)}, u32[]{:S(2)}, u32[]{:S(2)}) collective-permute-start(f32[16,512]{1,0:T(8,128)S(1)} %add_add_fusion.7.a), channel_id=1, source_target_pairs={{0,4},{1,5},{2,6},{3,7},{4,0},{5,1},{6,2},{7,3},{8,12},{9,13},{10,... | collective-permute-start | bytes 98312 | tf_op jit(solution)/shard_map/ppermute | solution.py:176
  28.0 4.8 %collective-permute-start.9 = (f32[16,512]{1,0:T(8,128)S(1)}, f32[16,512]{1,0:T(8,128)S(1)}, u32[]{:S(2)}, u32[]{:S(2)}) collective-permute-start(f32[16,512]{1,0:T(8,128)S(1)} %solve.4), channel_id=1, source_target_pairs={{0,3},{1,2},{2,1},{3,0},{4,7},{5,6},{6,5},{7,4},{8,11},{9,10},{10,... | collective-permute-start | bytes 98312 | tf_op jit(solution)/shard_map/ppermute | solution.py:176
  30.0 3.9 %collective-permute-start.7 = (f32[16,512]{1,0:T(8,128)S(1)}, f32[16,512]{1,0:T(8,128)S(1)}, u32[]{:S(2)}, u32[]{:S(2)}) collective-permute-start(f32[16,512]{1,0:T(8,128)S(1)} %solve.4), channel_id=1, source_target_pairs={{0,1},{1,0},{2,3},{3,2},{4,5},{5,4},{6,7},{7,6},{8,9},{9,8},{10,11... | collective-permute-start | bytes 98312 | tf_op jit(solution)/shard_map/ppermute | solution.py:176
  33.9 4.9 %collective-permute-start.10 = (f32[16,512]{1,0:T(8,128)S(1)}, f32[16,512]{1,0:T(8,128)S(1)}, u32[]{:S(2)}, u32[]{:S(2)}) collective-permute-start(f32[16,512]{1,0:T(8,128)S(1)} %add_add_fusion.6.a), channel_id=1, source_target_pairs={{0,4},{1,5},{2,6},{3,7},{4,0},{5,1},{6,2},{7,3},{8,12},{9,13},{10,... | collective-permute-start | bytes 98312 | tf_op jit(solution)/shard_map/ppermute | solution.py:176
  39.1 4.8 %collective-permute-start.16 = (f32[16,512]{1,0:T(8,128)S(1)}, f32[16,512]{1,0:T(8,128)S(1)}, u32[]{:S(2)}, u32[]{:S(2)}) collective-permute-start(f32[16,512]{1,0:T(8,128)S(1)} %get-tuple-element.37), channel_id=1, source_target_pairs={{0,3},{1,2},{2,1},{3,0},{4,7},{5,6},{6,5},{7,4},{8,11},{9,10},{10,... | collective-permute-start | bytes 98312 | tf_op jit(solution)/shard_map/ppermute | solution.py:176
  41.6 3.9 %collective-permute-start.15 = (f32[16,512]{1,0:T(8,128)S(1)}, f32[16,512]{1,0:T(8,128)S(1)}, u32[]{:S(2)}, u32[]{:S(2)}) collective-permute-start(f32[16,512]{1,0:T(8,128)S(1)} %get-tuple-element.37), channel_id=1, source_target_pairs={{0,2},{1,3},{2,0},{3,1},{4,6},{5,7},{6,4},{7,5},{8,10},{9,11},{10,... | collective-permute-start | bytes 98312 | tf_op jit(solution)/shard_map/ppermute | solution.py:176
  42.1 3.9 %collective-permute-start.14 = (f32[16,512]{1,0:T(8,128)S(1)}, f32[16,512]{1,0:T(8,128)S(1)}, u32[]{:S(2)}, u32[]{:S(2)}) collective-permute-start(f32[16,512]{1,0:T(8,128)S(1)} %get-tuple-element.37), channel_id=1, source_target_pairs={{0,1},{1,0},{2,3},{3,2},{4,5},{5,4},{6,7},{7,6},{8,9},{9,8},{10,11... | collective-permute-start | bytes 98312 | tf_op jit(solution)/shard_map/ppermute | solution.py:176
  46.0 4.9 %collective-permute-start.17 = (f32[16,512]{1,0:T(8,128)S(1)}, f32[16,512]{1,0:T(8,128)S(1)}, u32[]{:S(2)}, u32[]{:S(2)}) collective-permute-start(f32[16,512]{1,0:T(8,128)S(1)} %add_add_fusion.5.a), channel_id=1, source_target_pairs={{0,4},{1,5},{2,6},{3,7},{4,0},{5,1},{6,2},{7,3},{8,12},{9,13},{10,... | collective-permute-start | bytes 98312 | tf_op jit(solution)/shard_map/ppermute | solution.py:176
  52.0 5.0 %collective-permute-start.20 = (f32[16,512]{1,0:T(8,128)S(1)}, f32[16,512]{1,0:T(8,128)S(1)}, u32[]{:S(2)}, u32[]{:S(2)}) collective-permute-start(f32[16,512]{1,0:T(8,128)S(1)} %solve.5), channel_id=1, source_target_pairs={{0,3},{1,2},{2,1},{3,0},{4,7},{5,6},{6,5},{7,4},{8,11},{9,10},{10,... | collective-permute-start | bytes 98312 | tf_op jit(solution)/shard_map/ppermute | solution.py:176
  53.6 4.1 %collective-permute-start.19 = (f32[16,512]{1,0:T(8,128)S(1)}, f32[16,512]{1,0:T(8,128)S(1)}, u32[]{:S(2)}, u32[]{:S(2)}) collective-permute-start(f32[16,512]{1,0:T(8,128)S(1)} %solve.5), channel_id=1, source_target_pairs={{0,2},{1,3},{2,0},{3,1},{4,6},{5,7},{6,4},{7,5},{8,10},{9,11},{10,... | collective-permute-start | bytes 98312 | tf_op jit(solution)/shard_map/ppermute | solution.py:176
  57.9 4.9 %collective-permute-start.21 = (f32[16,512]{1,0:T(8,128)S(1)}, f32[16,512]{1,0:T(8,128)S(1)}, u32[]{:S(2)}, u32[]{:S(2)}) collective-permute-start(f32[16,512]{1,0:T(8,128)S(1)} %add_add_fusion.4.a), channel_id=1, source_target_pairs={{0,4},{1,5},{2,6},{3,7},{4,0},{5,1},{6,2},{7,3},{8,12},{9,13},{10,... | collective-permute-start | bytes 98312 | tf_op jit(solution)/shard_map/ppermute | solution.py:176
  63.0 4.9 %collective-permute-start.27 = (f32[16,512]{1,0:T(8,128)S(1)}, f32[16,512]{1,0:T(8,128)S(1)}, u32[]{:S(2)}, u32[]{:S(2)}) collective-permute-start(f32[16,512]{1,0:T(8,128)S(1)} %get-tuple-element.40), channel_id=1, source_target_pairs={{0,3},{1,2},{2,1},{3,0},{4,7},{5,6},{6,5},{7,4},{8,11},{9,10},{10,... | collective-permute-start | bytes 98312 | tf_op jit(solution)/shard_map/ppermute | solution.py:176
  70.0 4.9 %collective-permute-start.28 = (f32[16,512]{1,0:T(8,128)S(1)}, f32[16,512]{1,0:T(8,128)S(1)}, u32[]{:S(2)}, u32[]{:S(2)}) collective-permute-start(f32[16,512]{1,0:T(8,128)S(1)} %add_add_fusion.3.a), channel_id=1, source_target_pairs={{0,4},{1,5},{2,6},{3,7},{4,0},{5,1},{6,2},{7,3},{8,12},{9,13},{10,... | collective-permute-start | bytes 98312 | tf_op jit(solution)/shard_map/ppermute | solution.py:176
  76.0 5.2 %collective-permute-start.31 = (f32[16,512]{1,0:T(8,128)S(1)}, f32[16,512]{1,0:T(8,128)S(1)}, u32[]{:S(2)}, u32[]{:S(2)}) collective-permute-start(f32[16,512]{1,0:T(8,128)S(1)} %solve.6), channel_id=1, source_target_pairs={{0,3},{1,2},{2,1},{3,0},{4,7},{5,6},{6,5},{7,4},{8,11},{9,10},{10,... | collective-permute-start | bytes 98312 | tf_op jit(solution)/shard_map/ppermute | solution.py:176
  81.8 4.9 %collective-permute-start.32 = (f32[16,512]{1,0:T(8,128)S(1)}, f32[16,512]{1,0:T(8,128)S(1)}, u32[]{:S(2)}, u32[]{:S(2)}) collective-permute-start(f32[16,512]{1,0:T(8,128)S(1)} %add_add_fusion.2.a), channel_id=1, source_target_pairs={{0,4},{1,5},{2,6},{3,7},{4,0},{5,1},{6,2},{7,3},{8,12},{9,13},{10,... | collective-permute-start | bytes 98312 | tf_op jit(solution)/shard_map/ppermute | solution.py:176
  87.0 4.8 %collective-permute-start.38 = (f32[16,512]{1,0:T(8,128)S(1)}, f32[16,512]{1,0:T(8,128)S(1)}, u32[]{:S(2)}, u32[]{:S(2)}) collective-permute-start(f32[16,512]{1,0:T(8,128)S(1)} %get-tuple-element.43), channel_id=1, source_target_pairs={{0,3},{1,2},{2,1},{3,0},{4,7},{5,6},{6,5},{7,4},{8,11},{9,10},{10,... | collective-permute-start | bytes 98312 | tf_op jit(solution)/shard_map/ppermute | solution.py:176
  94.0 4.9 %collective-permute-start.39 = (f32[16,512]{1,0:T(8,128)S(1)}, f32[16,512]{1,0:T(8,128)S(1)}, u32[]{:S(2)}, u32[]{:S(2)}) collective-permute-start(f32[16,512]{1,0:T(8,128)S(1)} %add_add_fusion.1.a), channel_id=1, source_target_pairs={{0,4},{1,5},{2,6},{3,7},{4,0},{5,1},{6,2},{7,3},{8,12},{9,13},{10,... | collective-permute-start | bytes 98312 | tf_op jit(solution)/shard_map/ppermute | solution.py:176
  99.9 4.8 %collective-permute-start.42 = (f32[16,512]{1,0:T(8,128)S(1)}, f32[16,512]{1,0:T(8,128)S(1)}, u32[]{:S(2)}, u32[]{:S(2)}) collective-permute-start(f32[16,512]{1,0:T(8,128)S(1)} %solve.7), channel_id=1, source_target_pairs={{0,3},{1,2},{2,1},{3,0},{4,7},{5,6},{6,5},{7,4},{8,11},{9,10},{10,... | collective-permute-start | bytes 98312 | tf_op jit(solution)/shard_map/ppermute | solution.py:176
  103.4 5.2 %collective-permute-start.13 = (f32[16,512]{1,0:T(8,128)S(1)}, f32[16,512]{1,0:T(8,128)S(1)}, u32[]{:S(2)}, u32[]{:S(2)}) collective-permute-start(f32[16,512]{1,0:T(8,128)S(1)} %get-tuple-element.36.refs_0_), channel_id=1, source_target_pairs={{0,24},{8,16},{16,8},{24,0},{1,25},{9,17},{17,9},{25,1},{2,26},{10... | collective-permute-start | bytes 98312 | tf_op jit(solution)/shard_map/ppermute | solution.py:176
  103.4 6.6 %collective-permute-start.12 = (f32[16,512]{1,0:T(8,128)S(1)}, f32[16,512]{1,0:T(8,128)S(1)}, u32[]{:S(2)}, u32[]{:S(2)}) collective-permute-start(f32[16,512]{1,0:T(8,128)S(1)} %get-tuple-element.36.refs_0_), channel_id=1, source_target_pairs={{0,16},{8,24},{16,0},{24,8},{1,17},{9,25},{17,1},{25,9},{2,18},{10... | collective-permute-start | bytes 98312 | tf_op jit(solution)/shard_map/ppermute | solution.py:176
  104.8 5.3 %collective-permute-start.11 = (f32[16,512]{1,0:T(8,128)S(1)}, f32[16,512]{1,0:T(8,128)S(1)}, u32[]{:S(2)}, u32[]{:S(2)}) collective-permute-start(f32[16,512]{1,0:T(8,128)S(1)} %get-tuple-element.36.refs_0_), channel_id=1, source_target_pairs={{0,8},{8,0},{16,24},{24,16},{1,9},{9,1},{17,25},{25,17},{2,10},{10... | collective-permute-start | bytes 98312 | tf_op jit(solution)/shard_map/ppermute | solution.py:176
  105.7 5.1 %collective-permute-start.24 = (f32[16,512]{1,0:T(8,128)S(1)}, f32[16,512]{1,0:T(8,128)S(1)}, u32[]{:S(2)}, u32[]{:S(2)}) collective-permute-start(f32[16,512]{1,0:T(8,128)S(1)} %get-tuple-element.39.refs_4_), channel_id=1, source_target_pairs={{0,24},{8,16},{16,8},{24,0},{1,25},{9,17},{17,9},{25,1},{2,26},{10... | collective-permute-start | bytes 98312 | tf_op jit(solution)/shard_map/ppermute | solution.py:176
  105.8 6.3 %collective-permute-start.43 = (f32[16,512]{1,0:T(8,128)S(1)}, f32[16,512]{1,0:T(8,128)S(1)}, u32[]{:S(2)}, u32[]{:S(2)}) collective-permute-start(f32[16,512]{1,0:T(8,128)S(1)} %add_add_fusion.a), channel_id=1, source_target_pairs={{0,4},{1,5},{2,6},{3,7},{4,0},{5,1},{6,2},{7,3},{8,12},{9,13},{10,... | collective-permute-start | bytes 98312 | tf_op jit(solution)/shard_map/ppermute | solution.py:176
  108.7 3.9 %collective-permute-start.23 = (f32[16,512]{1,0:T(8,128)S(1)}, f32[16,512]{1,0:T(8,128)S(1)}, u32[]{:S(2)}, u32[]{:S(2)}) collective-permute-start(f32[16,512]{1,0:T(8,128)S(1)} %get-tuple-element.39.refs_4_), channel_id=1, source_target_pairs={{0,16},{8,24},{16,0},{24,8},{1,17},{9,25},{17,1},{25,9},{2,18},{10... | collective-permute-start | bytes 98312 | tf_op jit(solution)/shard_map/ppermute | solution.py:176
  110.1 4.3 %collective-permute-start.35 = (f32[16,512]{1,0:T(8,128)S(1)}, f32[16,512]{1,0:T(8,128)S(1)}, u32[]{:S(2)}, u32[]{:S(2)}) collective-permute-start(f32[16,512]{1,0:T(8,128)S(1)} %get-tuple-element.42.refs_8_), channel_id=1, source_target_pairs={{0,24},{8,16},{16,8},{24,0},{1,25},{9,17},{17,9},{25,1},{2,26},{10... | collective-permute-start | bytes 98312 | tf_op jit(solution)/shard_map/ppermute | solution.py:176
  110.8 4.8 %collective-permute-start.34 = (f32[16,512]{1,0:T(8,128)S(1)}, f32[16,512]{1,0:T(8,128)S(1)}, u32[]{:S(2)}, u32[]{:S(2)}) collective-permute-start(f32[16,512]{1,0:T(8,128)S(1)} %get-tuple-element.42.refs_8_), channel_id=1, source_target_pairs={{0,16},{8,24},{16,0},{24,8},{1,17},{9,25},{17,1},{25,9},{2,18},{10... | collective-permute-start | bytes 98312 | tf_op jit(solution)/shard_map/ppermute | solution.py:176
  113.2 6.3 %collective-permute-start.46 = (f32[16,512]{1,0:T(8,128)S(1)}, f32[16,512]{1,0:T(8,128)S(1)}, u32[]{:S(2)}, u32[]{:S(2)}) collective-permute-start(f32[16,512]{1,0:T(8,128)S(1)} %get-tuple-element.45.refs_12_), channel_id=1, source_target_pairs={{0,24},{8,16},{16,8},{24,0},{1,25},{9,17},{17,9},{25,1},{2,26},{10... | collective-permute-start | bytes 98312 | tf_op jit(solution)/shard_map/ppermute | solution.py:176
  114.3 5.1 %collective-permute-start.45 = (f32[16,512]{1,0:T(8,128)S(1)}, f32[16,512]{1,0:T(8,128)S(1)}, u32[]{:S(2)}, u32[]{:S(2)}) collective-permute-start(f32[16,512]{1,0:T(8,128)S(1)} %get-tuple-element.45.refs_12_), channel_id=1, source_target_pairs={{0,16},{8,24},{16,0},{24,8},{1,17},{9,25},{17,1},{25,9},{2,18},{10... | collective-permute-start | bytes 98312 | tf_op jit(solution)/shard_map/ppermute | solution.py:176
  (27 other events, 108.4 us)

commit v2 on v1

v2 whole, which is shorter than its diff:
```python
import functools

import jax
import jax.numpy as jnp
from jax import lax
from jax.experimental import pallas as pl
from jax.experimental.pallas import tpu as pltpu
from jax.sharding import PartitionSpec as P

centre_weight = 128.0 / 30.0
face_weight = 14.0 / 30.0
edge_weight = 3.0 / 30.0
corner_weight = 1.0 / 30.0

VMEM = pl.BlockSpec(memory_space=pltpu.VMEM)
SMEM = pl.BlockSpec(memory_space=pltpu.SMEM)
F32 = jnp.float32
BF16 = jnp.bfloat16


def params():
    return pltpu.CompilerParams(vmem_limit_bytes=16 << 20)


def cost(flops, moved):
    return pl.CostEstimate(flops=flops, bytes_accessed=moved, transcendentals=0)


def dot_nt(a, b):
    return lax.dot_general(a, b, (((1,), (1,)), ((), ())), preferred_element_type=F32)


def split3(x):
    high = x.astype(BF16)
    rest = x - high.astype(F32)
    middle = rest.astype(BF16)
    low = (rest - middle.astype(F32)).astype(BF16)
    return high, middle, low


def split2(x):
    high = x.astype(BF16)
    return high, (x - high.astype(F32)).astype(BF16)


def select_columns(x, chosen):
    count = x.shape[0]
    parts = dot_nt(jnp.concatenate(split3(x), axis=0), chosen)
    return (parts[2 * count :] + parts[count : 2 * count]) + parts[:count]


def rows_of(index, size, total):
    return pl.ds(pl.multiple_of((index & (total // size - 1)) * size, 8), size)


def leaf_kernel(gx, gy, lanes, blocks, field, source, wave, cmap, front, residual, *rest):
    chunks, face, coupled = rest[:lanes], rest[lanes], rest[lanes + 1]
    step = pl.program_id(0)
    rows = field.shape[0]
    cells = gx * gy
    here = rows // cells
    width = field.shape[1]
    v = field[...]
    row = lax.broadcasted_iota(jnp.int32, (rows, width), 0) % cells
    lane = lax.broadcasted_iota(jnp.int32, (rows, width), 1)
    zero = jnp.zeros_like(v)
    left = jnp.where(lane > 0, pltpu.roll(v, 1, 1), zero)
    right = jnp.where(lane < width - 1, pltpu.roll(v, width - 1, 1), zero)
    sides = left + right
    once = face_weight * v + edge_weight * sides
    twice = edge_weight * v + corner_weight * sides
    y = row % gy

    def shift_y(p):
        below = jnp.where(y > 0, pltpu.roll(p, 1, 0), zero)
        above = jnp.where(y < gy - 1, pltpu.roll(p, rows - 1, 0), zero)
        return below + above

    around = once + shift_y(twice)
    below = jnp.where(row >= gy, pltpu.roll(around, gy, 0), zero)
    above = jnp.where(row < cells - gy, pltpu.roll(around, rows - gy, 0), zero)
    beside = face_weight * sides + shift_y(once) + (below + above)
    weight = centre_weight - wave[...]
    centre = (v.reshape(here, cells, width) * weight[None]).reshape(rows, width)
    residual[...] = source[...] - (centre - beside)
    for j in range(gy):
        face[pl.ds(step * here, here), j * width : (j + 1) * width] = residual[
            pl.ds(cells - gy + j, here, stride=cells), :
        ]

    @pl.when(step == blocks - 1)
    def _():
        slots = coupled.shape[1]
        hits = lax.broadcasted_iota(jnp.int32, (slots, cmap.shape[1]), 0) == cmap[...]
        coupled[...] = face_weight * select_columns(face[...], hits.astype(BF16))
        me = lax.axis_index("leaf")
        size = chunks[0].shape[0]
        for m in range(lanes):
            rows_there = rows_of(me ^ m, size, coupled.shape[0])
            chunk = coupled[rows_there, :]
            chunks[m][...] = chunk if m else chunk + front[rows_there, :]


def picker(order, panel, width):
    rows = order.shape[1]
    wanted = lax.broadcasted_iota(jnp.int32, (width, rows), 0) + panel * width
    return (wanted == order).astype(BF16)


def prelude_kernel(quarters, panels, inverse, lower, order, slot, under, held, sems):
    width = inverse.shape[1]
    size = width // quarters
    start = (lax.axis_index("leaf") & (quarters - 1)) * size
    copies = [pltpu.make_async_copy(inverse.at[pl.ds(pl.multiple_of(start, size), size), :], slot, sems.at[0])]
    for panel in range(panels - 1):
        rows = pl.ds(pl.multiple_of(panel * width + start, size), size)
        copies.append(pltpu.make_async_copy(lower.at[rows, :], held.at[panel], sems.at[panel + 1]))
    for copy in copies:
        copy.start()
    own = order[...]
    under[size:, :] = jnp.broadcast_to(own.astype(F32), (8, own.shape[1]))
    total = jnp.zeros(held.shape[1:], F32)
    for panel in range(panels - 1):
        copies[panel + 1].wait()
        here = (own >= (panel + 1) * width) & (own < (panel + 2) * width)
        total = total + jnp.where(here, held[panel].astype(F32), jnp.zeros_like(total))
    under[:size, :] = total
    copies[0].wait()


def pack_kernel(*refs):
    out = refs[-1]
    width = refs[0].shape[1]
    for i, piece in enumerate(refs[:-1]):
        out[:, i * width : (i + 1) * width] = piece[: out.shape[0], :]


def under_kernel(*refs):
    pieces, out = refs[:-1], refs[-1]
    size = pieces[0].shape[0]
    me = lax.axis_index("leaf") & (len(pieces) - 1)
    for k, piece in enumerate(pieces):
        out[pl.ds(pl.multiple_of((me ^ k) * size, size), size), :] = piece[...].astype(BF16)


def slots_kernel(quarters, inverse, *refs):
    pieces, (high, middle) = refs[:-2], refs[-2:]
    me = lax.axis_index("leaf") & (quarters - 1)
    high[0], middle[0] = split2(inverse[...])
    for i, piece in enumerate(pieces):
        size = piece.shape[0]
        rows = pl.ds(pl.multiple_of((me ^ (i % quarters)) * size, size), size)
        high[i // quarters + 1, rows, :], middle[i // quarters + 1, rows, :] = split2(piece[...])


def first_kernel(*refs):
    chunks, reduced = refs[:-1], refs[-1]
    total = chunks[0][...]
    for chunk in chunks[1:]:
        total = total + chunk[...]
    reduced[...] = total


def solve_share(panel, near, rows, orders, high, middle, owners, out):
    count = rows.shape[0]
    width = out.shape[1]
    wanted = lax.broadcasted_iota(jnp.int32, (width, orders.shape[1]), 0) + panel * width
    chosen = (wanted == orders).astype(BF16)
    block = dot_nt(jnp.concatenate(split2(rows), axis=0), chosen).astype(BF16)
    apart = owners[panel] ^ lax.axis_index("front")
    slot = apart // near
    first = dot_nt(block, high[slot])
    second = dot_nt(block[:count], middle[slot])
    solved = (second + first[count:]) + first[:count]
    holds = (apart & (near - 1)) == 0
    out[...] = jnp.where(holds, solved, jnp.zeros_like(solved))


def begin_kernel(near, size, *refs):
    rows, own, under = refs[:near], refs[near], refs[near + 1 : 2 * near]
    high, middle, owners, orders, out = refs[2 * near :]
    orders[...] = jnp.concatenate(
        [own[...]] + [x[size : size + 1, :].astype(jnp.int32) for x in under], axis=1
    )
    values = jnp.concatenate([x[...] for x in rows], axis=1)
    solve_share(0, near, values, orders[...], high, middle, owners, out)


def join_kernel(a, b, reduced, out):
    width = a.shape[1]
    out[:, :width] = a[...] + b[...]
    out[:, width:] = reduced[...]


def updated(panel, half, lower, order, reduced):
    update = jnp.dot(half, lower[...], preferred_element_type=F32)
    keep = order >= (panel + 1) * half.shape[1]
    return reduced[...] - jnp.where(keep, update, jnp.zeros_like(update))


def step_kernel(panel, near, loose, *refs):
    parts, refs = refs[:near], refs[near:]
    others, refs = refs[:loose], refs[loose:]
    lower, below, orders, reduced_in, high, middle, owners = refs[:7]
    earlier, (solved, reduced, out) = refs[7:-3], refs[-3:]
    width = out.shape[1]
    rows_here = reduced.shape[1]
    p = [x[:, :width] for x in parts]
    block = (p[0] + p[1]) + (p[2] + p[3])
    for i, x in enumerate(earlier):
        solved[:, i * width : (i + 1) * width] = x[...]
    solved[:, len(earlier) * width :] = block
    half = block.astype(BF16)
    left = updated(panel, half, lower, orders[:, :rows_here], reduced_in)
    reduced[...] = left
    values = [x[...] for x in others] if loose else [x[:, width:] for x in parts[1:]]
    values = jnp.concatenate(values, axis=1)
    values = values - jnp.dot(half, below[...], preferred_element_type=F32)
    rows = jnp.concatenate([left, values], axis=1)
    solve_share(panel + 1, near, rows, orders[...], high, middle, owners, out)


def last_kernel(panel, near, *refs):
    parts, lower, orders, reduced_in, out = refs[:near], *refs[near : near + 3], refs[-1]
    width = lower.shape[0]
    p = [x[:, :width] for x in parts]
    block = (p[0] + p[1]) + (p[2] + p[3])
    out[:, :width] = block
    out[:, width:] = updated(panel, block.astype(BF16), lower, orders[:, : out.shape[1] - width], reduced_in)


def gather_kernel(groups, *refs):
    early, late = refs[:groups], refs[groups : 2 * groups]
    solved, reduced = refs[2 * groups :]
    me = lax.axis_index("leaf")
    size, ahead = early[0].shape
    width = solved.shape[1] - ahead
    for m in range(groups):
        rows = rows_of(me ^ m, size, solved.shape[0])
        solved[rows, :ahead] = early[m][...]
        solved[rows, ahead:] = late[m][:, :width]
        reduced[rows, :] = late[m][:, width:]


def per_device(
    lanes,
    fronts,
    leaf_field,
    leaf_source,
    wave_squared,
    coupling_map,
    front_rhs,
    row_order,
    lower_panels,
    inverse_slots,
    panel_owners,
):
    rhs_count, gx, gy, gz = leaf_field.shape
    cells = gx * gy
    rows_here = front_rhs.shape[1]
    width = inverse_slots.shape[1]
    panels = lower_panels.shape[0] // width
    groups = min(lanes, rhs_count // 8)
    share = rhs_count // groups

    near, quarters = 4, 4
    far = fronts // near

    def trade(x, axis, count, mask):
        return lax.ppermute(x, axis, [(i, i ^ mask) for i in range(count)])

    def across(x):
        mask = near
        while mask * 2 < fronts:
            x = x + trade(x, "front", fronts, mask)
            mask *= 2
        return x, trade(x, "front", fronts, mask)

    def nearby(x):
        r = {m: trade(x, "front", fronts, m) for m in reversed(range(1, near))}
        return [x] + [r[m] for m in range(1, near)]

    def call(kernel, name, operands, out_shape, in_specs=None, **kw):
        many = isinstance(out_shape, list)
        return pl.pallas_call(
            kernel,
            in_specs=in_specs or [VMEM] * len(operands),
            out_specs=[VMEM] * len(out_shape) if many else VMEM,
            out_shape=out_shape,
            compiler_params=kw.pop("compiler_params", params()),
            name=name,
            **kw,
        )(*operands)

    def f32(*shape):
        return jax.ShapeDtypeStruct(shape, F32)

    def bf16(*shape):
        return jax.ShapeDtypeStruct(shape, BF16)

    blocks = 4
    rows = rhs_count * cells
    field = leaf_field.reshape(rows, gz)
    source = leaf_source.reshape(rows, gz)
    wave = wave_squared.reshape(cells, gz)
    order = row_order.reshape(1, rows_here)
    size = width // quarters
    anywhere = pl.BlockSpec(memory_space=pl.ANY)

    slot, under = call(
        functools.partial(prelude_kernel, quarters, panels),
        "prelude",
        (inverse_slots, lower_panels, order),
        [f32(size, width), f32(size + 8, rows_here)],
        [anywhere, anywhere, VMEM],
        scratch_shapes=[
            pltpu.VMEM((panels - 1, size, rows_here), BF16),
            pltpu.SemaphoreType.DMA((panels,)),
        ],
        compiler_params=None,
    )
    slots = [trade(slot, "front", fronts, near * m) for m in range(1, far)]
    unders = nearby(under)[1:]

    piece, block_shape = f32(share, rows_here), f32(share, width)
    tile = pl.BlockSpec((rows // blocks, gz), lambda i: (i, 0))
    whole = lambda shape: pl.BlockSpec(shape, lambda i: (0,) * len(shape))
    residual, *chunks = pl.pallas_call(
        functools.partial(leaf_kernel, gx, gy, lanes, blocks),
        grid=(blocks,),
        in_specs=[tile, tile] + [whole(x.shape) for x in (wave, coupling_map, front_rhs)],
        out_specs=[tile] + [whole(piece.shape)] * lanes,
        out_shape=[f32(rows, gz)] + [piece] * lanes,
        scratch_shapes=[
            pltpu.VMEM((rhs_count, gy * gz), F32),
            pltpu.VMEM((rhs_count, rows_here), F32),
        ],
        compiler_params=params(),
        cost_estimate=cost(40 * rows * gz, 12 * rows * gz),
        name="leaf",
    )(field, source, wave, coupling_map, front_rhs)
    chunks = [chunks[0]] + [trade(chunks[m], "leaf", lanes, m) for m in range(1, lanes)]
    reduced = call(first_kernel, "first", chunks, piece)
    groups_rows = nearby(reduced)

    def all_quarters(x):
        y = trade(x, "leaf", lanes, 2)
        return [x, trade(x, "leaf", lanes, 1), y, trade(y, "leaf", lanes, 1)]

    pieces = [q for x in slots for q in all_quarters(x)]
    high, middle = call(
        functools.partial(slots_kernel, quarters),
        "slots",
        (inverse_slots, *pieces),
        [bf16(far, *inverse_slots.shape)] * 2,
    )
    packed = call(pack_kernel, "pack", unders, f32(size, (near - 1) * rows_here))
    below = call(under_kernel, "under", all_quarters(packed), bf16(width, (near - 1) * rows_here))

    orders, own = call(
        functools.partial(begin_kernel, near, size),
        "begin",
        (*groups_rows, order, *unders, high, middle, panel_owners),
        [jax.ShapeDtypeStruct((1, near * rows_here), jnp.int32), block_shape],
        [VMEM] * (2 * near + 2) + [SMEM],
    )
    solved_list, early = [], []
    for panel in range(panels):
        lower = lower_panels[panel * width : (panel + 1) * width]
        a, b = across(own)
        if panel == 0:
            parts, loose = nearby(a + b), groups_rows[1:]
        else:
            joined = call(join_kernel, "join", (a, b, reduced), f32(share, width + rows_here))
            parts, loose = nearby(joined), []
        if panel == panels - 1:
            late = call(
                functools.partial(last_kernel, panel, near),
                "last",
                (*parts, lower, orders, reduced, *early[1:]),
                f32(share, width + rows_here),
                [VMEM] * (near + 3) + [anywhere] * len(early[1:]),
            )
            continue
        pack = panel == panels - 2
        earlier = solved_list if pack else []
        operands = (*parts, *loose, lower, below, orders, reduced, high, middle)
        solved, reduced, own = call(
            functools.partial(step_kernel, panel, near, len(loose)),
            "step",
            (*operands, panel_owners, *earlier),
            [f32(share, width * (len(earlier) + 1)), piece, block_shape],
            [VMEM] * len(operands) + [SMEM] + [VMEM] * len(earlier),
        )
        solved_list.append(solved)
        if pack:
            early = [solved] + [trade(solved, "leaf", lanes, m) for m in range(1, groups)]
    late = [late] + [trade(late, "leaf", lanes, m) for m in range(1, groups)]
    solved, reduced = call(
        functools.partial(gather_kernel, groups),
        "collect",
        (*early, *late),
        [f32(rhs_count, panels * width), f32(rhs_count, rows_here)],
    )
    return (residual.reshape(leaf_field.shape), solved, reduced)


def solution(mesh):
    return jax.shard_map(
        functools.partial(per_device, mesh.shape["leaf"], mesh.shape["front"]),
        mesh=mesh,
        in_specs=(
            P(None, ("leaf", "front"), None, None),
            P(None, ("leaf", "front"), None, None),
            P(("leaf", "front"), None, None),
            P(("leaf", "front"), None),
            P(None, "front"),
            P("front"),
            P(None, "front"),
            P("front", None),
            P(),
        ),
        out_specs=(P(None, ("leaf", "front"), None, None), P(), P(None, "front")),
        check_vma=False,
    )
```

time: 121 us -> 116 us (0.959)
  starting transfers between devices: 61.7 us -> 47.6 us
  waiting for transfers between devices: 43 us -> 55 us
  local copies, waits for them, and re-layouts: 5.79 us -> 0.79 us
  Pallas kernels: 8.97 us -> 11.9 us
    ppermute x50 -> x38, starting transfers between devices: 61.7 us -> 47.6 us  [trade(): return lax.ppermute(x, axis, [(i, i ^ mask) for i in range(count)])]
    ppermute x50 -> x38, waiting for transfers between devices: 43 us -> 55 us  [trade(): return lax.ppermute(x, axis, [(i, i ^ mask) for i in range(count)])]
    unnamed x18, local copies, waits for them, and re-layouts: 5.72 us -> 0.72 us
    pallas_call x11 -> x14, Pallas kernels: 6.57 us -> 9.5 us  [call(): pl.pallas_call(kernel, in_specs=in_specs or [VMEM] * len(operands), out_s...]
  transfers between devices with their start and end apart: 50 -> 38, of which waited for: 34 -> 26; matrix products, arithmetic and copies ran while one was open for 0% -> 0% of each run, Pallas kernels for 0% -> 4%
where the time goes in v2:
time: 116 us
  waiting for transfers between devices  55 us (47%)
  starting transfers between devices  47.6 us (41%)
  Pallas kernels  11.9 us (10%)
    ppermute x38, waiting for transfers between devices, trade(): return lax.ppermute(x, axis, [(i, i ^ mask) for i in range(count)])  55 us
    ppermute x38, starting transfers between devices, trade(): return lax.ppermute(x, axis, [(i, i ^ mask) for i in range(count)])  47.6 us
    pallas_call x14, Pallas kernels, call(): pl.pallas_call(kernel, in_specs=in_specs or [VMEM] * len(operands), out_s...  9.5 us
    pallas_call x1, Pallas kernels, per_device(): pl.pallas_call(functools.partial(leaf_kernel, gx, gy, lanes, blocks), gri...  2.43 us
  transfers between devices with their start and end apart: 38, of which 26 were waited for; matrix products, arithmetic and copies ran while one was open for 0% of the time, Pallas kernels for 4%

profile of v2, /device:TPU:0, one launch (start us, length us, event | category | flops | bytes accessed | tf_op | source)
XLA Modules:
  0.0 116.1 jit_solution(17471039231717558148)
XLA Ops:
  0.7 2.5 %prelude.1 = (f32[128,512]{1,0:T(8,128)}, f32[136,256]{1,0:T(8,128)}) custom-call(f32[512,512]{1,0:T(8,128)} %inverse.3, bf16[2048,256]{1,0:T(8,128)(2,1)} %lower.1, s32[1,256]{1,0:T(1,128)} %bitcast.8), custom_call_target="tpu_custom_call" | custom-call | tf_op jit(solution)/shard_map/prelude/pallas_call | solution.py:285
  3.2 4.1 %collective-permute-start.9 = (f32[128,512]{1,0:T(8,128)}, f32[128,512]{1,0:T(8,128)S(1)}, u32[]{:S(2)}, u32[]{:S(2)}) collective-permute-start(f32[128,512]{1,0:T(8,128)} %get-tuple-element.31), channel_id=1, source_target_pairs={{0,4},{1,5},{2,6},{3,7},{4,0},{5,1},{6,2},{7,3},{8,12},{9,13},{10,... | collective-permute-start | bytes 786440 | tf_op jit(solution)/shard_map/ppermute | solution.py:270
  7.4 1.5 %collective-permute-start.6 = (f32[136,256]{1,0:T(8,128)}, f32[136,256]{1,0:T(8,128)S(1)}, u32[]{:S(2)}, u32[]{:S(2)}) collective-permute-start(f32[136,256]{1,0:T(8,128)} %get-tuple-element.30), channel_id=1, source_target_pairs={{0,1},{1,0},{2,3},{3,2},{4,5},{5,4},{6,7},{7,6},{8,9},{9,8},{10,11... | collective-permute-start | bytes 417800 | tf_op jit(solution)/shard_map/ppermute | solution.py:270
  8.9 1.6 %collective-permute-start.7 = (f32[136,256]{1,0:T(8,128)}, f32[136,256]{1,0:T(8,128)S(1)}, u32[]{:S(2)}, u32[]{:S(2)}) collective-permute-start(f32[136,256]{1,0:T(8,128)} %get-tuple-element.30), channel_id=1, source_target_pairs={{0,2},{1,3},{2,0},{3,1},{4,6},{5,7},{6,4},{7,5},{8,10},{9,11},{10,... | collective-permute-start | bytes 417800 | tf_op jit(solution)/shard_map/ppermute | solution.py:270
  10.9 8.7 %collective-permute-done.9.refs_0_ = f32[128,512]{1,0:T(8,128)S(1)} collective-permute-done((f32[128,512]{1,0:T(8,128)}, f32[128,512]{1,0:T(8,128)S(1)}, u32[]{:S(2)}, u32[]{:S(2)}) %collective-permute-start.9) | collective-permute-done | bytes 262176 | tf_op jit(solution)/shard_map/ppermute | solution.py:270
  19.6 1.5 %collective-permute-start.11 = (f32[128,512]{1,0:T(8,128)S(1)}, f32[128,512]{1,0:T(8,128)S(1)}, u32[]{:S(2)}, u32[]{:S(2)}) collective-permute-start(f32[128,512]{1,0:T(8,128)S(1)} %collective-permute-done.9.refs_0_), channel_id=1, source_target_pairs={{0,16},{8,24},{16,0},{24,8},{1,17},{9,25},{17,1},{25,9},{2,18},{10... | collective-permute-start | bytes 786440 | tf_op jit(solution)/shard_map/ppermute | solution.py:270
  21.6 1.6 %collective-permute-start.18 = (f32[128,768]{1,0:T(8,128)S(1)}, f32[128,768]{1,0:T(8,128)S(1)}, u32[]{:S(2)}, u32[]{:S(2)}) collective-permute-start(f32[128,768]{1,0:T(8,128)S(1)} %pack.1.refs_0_), channel_id=1, source_target_pairs={{0,16},{8,24},{16,0},{24,8},{1,17},{9,25},{17,1},{25,9},{2,18},{10... | collective-permute-start | bytes 1179656 | tf_op jit(solution)/shard_map/ppermute | solution.py:270
  23.2 5.6 %collective-permute-done.11.refs_2_ = f32[128,512]{1,0:T(8,128)S(1)} collective-permute-done((f32[128,512]{1,0:T(8,128)S(1)}, f32[128,512]{1,0:T(8,128)S(1)}, u32[]{:S(2)}, u32[]{:S(2)}) %collective-permute-start.11) | collective-permute-done | bytes 262176 | tf_op jit(solution)/shard_map/ppermute | solution.py:270
  29.3 6.2 %collective-permute-done.18.refs_2_ = f32[128,768]{1,0:T(8,128)S(1)} collective-permute-done((f32[128,768]{1,0:T(8,128)S(1)}, f32[128,768]{1,0:T(8,128)S(1)}, u32[]{:S(2)}, u32[]{:S(2)}) %collective-permute-start.18) | collective-permute-done | bytes 393248 | tf_op jit(solution)/shard_map/ppermute | solution.py:270
  35.5 2.4 %leaf.1 = (f32[1024,128]{1,0:T(8,128)}, f32[16,256]{1,0:T(8,128)S(1)}, f32[16,256]{1,0:T(8,128)S(1)}, f32[16,256]{1,0:T(8,128)S(1)}, f32[16,256]{1,0:T(8,128)S(1)}) custom-call(f32[1024,128]{1,0:T(8,128)S(1)} %bitcast.5, f32[1024,128]{1,0:T(8,128)S(1)} %bitcast.6, f32[16,128]{1,0:T(8,128)S(1)} %bitcast.7, s32[1,512]{1,0:T(1,128)S(1)} %copy-done.7, ...), custom_call_target="tpu_custom_call" | custom-call | flops 5242880 | bytes 1572864 | tf_op jit(solution)/shard_map/leaf/pallas_call | solution.py:328
  40.5 2.4 %collective-permute-done.1.refs_2_ = f32[16,256]{1,0:T(8,128)S(1)} collective-permute-done((f32[16,256]{1,0:T(8,128)S(1)}, f32[16,256]{1,0:T(8,128)S(1)}, u32[]{:S(2)}, u32[]{:S(2)}) %collective-permute-start.1) | collective-permute-done | bytes 16416 | tf_op jit(solution)/shard_map/ppermute | solution.py:270
  43.1 3.1 %collective-permute-done.2.refs_3_ = f32[16,256]{1,0:T(8,128)S(1)} collective-permute-done((f32[16,256]{1,0:T(8,128)S(1)}, f32[16,256]{1,0:T(8,128)S(1)}, u32[]{:S(2)}, u32[]{:S(2)}) %collective-permute-start.2) | collective-permute-done | bytes 16416 | tf_op jit(solution)/shard_map/ppermute | solution.py:270
  47.6 1.7 %collective-permute-start.4 = (f32[16,256]{1,0:T(8,128)S(1)}, f32[16,256]{1,0:T(8,128)S(1)}, u32[]{:S(2)}, u32[]{:S(2)}) collective-permute-start(f32[16,256]{1,0:T(8,128)S(1)} %first.1.refs_0_.refs_10_), channel_id=1, source_target_pairs={{0,2},{1,3},{2,0},{3,1},{4,6},{5,7},{6,4},{7,5},{8,10},{9,11},{10,... | collective-permute-start | bytes 49160 | tf_op jit(solution)/shard_map/ppermute | solution.py:270
  51.4 2.6 %collective-permute-done.5.refs_3_.refs_6_ = f32[16,256]{1,0:T(8,128)S(1)} collective-permute-done((f32[16,256]{1,0:T(8,128)S(1)}, f32[16,256]{1,0:T(8,128)S(1)}, u32[]{:S(2)}, u32[]{:S(2)}) %collective-permute-start.5) | collective-permute-done | bytes 16416 | tf_op jit(solution)/shard_map/ppermute | solution.py:270
  56.0 3.3 %collective-permute-start.13 = (f32[16,512]{1,0:T(8,128)S(1)}, f32[16,512]{1,0:T(8,128)S(1)}, u32[]{:S(2)}, u32[]{:S(2)}) collective-permute-start(f32[16,512]{1,0:T(8,128)S(1)} %get-tuple-element.34), channel_id=1, source_target_pairs={{0,4},{1,5},{2,6},{3,7},{4,0},{5,1},{6,2},{7,3},{8,12},{9,13},{10,... | collective-permute-start | bytes 98312 | tf_op jit(solution)/shard_map/ppermute | solution.py:270
  59.3 1.9 %collective-permute-done.13 = f32[16,512]{1,0:T(8,128)S(1)} collective-permute-done((f32[16,512]{1,0:T(8,128)S(1)}, f32[16,512]{1,0:T(8,128)S(1)}, u32[]{:S(2)}, u32[]{:S(2)}) %collective-permute-start.13) | collective-permute-done | bytes 32800 | tf_op jit(solution)/shard_map/ppermute | solution.py:270
  61.9 2.8 %collective-permute-start.16 = (f32[16,512]{1,0:T(8,128)S(1)}, f32[16,512]{1,0:T(8,128)S(1)}, u32[]{:S(2)}, u32[]{:S(2)}) collective-permute-start(f32[16,512]{1,0:T(8,128)S(1)} %add.3.refs_0_), channel_id=1, source_target_pairs={{0,3},{1,2},{2,1},{3,0},{4,7},{5,6},{6,5},{7,4},{8,11},{9,10},{10,... | collective-permute-start | bytes 98312 | tf_op jit(solution)/shard_map/ppermute | solution.py:270
  68.3 2.9 %collective-permute-start.20 = (f32[16,512]{1,0:T(8,128)S(1)}, f32[16,512]{1,0:T(8,128)S(1)}, u32[]{:S(2)}, u32[]{:S(2)}) collective-permute-start(f32[16,512]{1,0:T(8,128)S(1)} %get-tuple-element.36.a), channel_id=1, source_target_pairs={{0,4},{1,5},{2,6},{3,7},{4,0},{5,1},{6,2},{7,3},{8,12},{9,13},{10,... | collective-permute-start | bytes 98312 | tf_op jit(solution)/shard_map/ppermute | solution.py:270
  71.3 1.9 %collective-permute-done.20.b = f32[16,512]{1,0:T(8,128)S(1)} collective-permute-done((f32[16,512]{1,0:T(8,128)S(1)}, f32[16,512]{1,0:T(8,128)S(1)}, u32[]{:S(2)}, u32[]{:S(2)}) %collective-permute-start.20) | collective-permute-done | bytes 32800 | tf_op jit(solution)/shard_map/ppermute | solution.py:270
  74.3 2.0 %collective-permute-start.22 = (f32[16,768]{1,0:T(8,128)S(1)}, f32[16,768]{1,0:T(8,128)S(1)}, u32[]{:S(2)}, u32[]{:S(2)}) collective-permute-start(f32[16,768]{1,0:T(8,128)S(1)} %join.3.refs_0_), channel_id=1, source_target_pairs={{0,2},{1,3},{2,0},{3,1},{4,6},{5,7},{6,4},{7,5},{8,10},{9,11},{10,... | collective-permute-start | bytes 147464 | tf_op jit(solution)/shard_map/ppermute | solution.py:270
  78.4 2.9 %collective-permute-done.23.refs_3_ = f32[16,768]{1,0:T(8,128)S(1)} collective-permute-done((f32[16,768]{1,0:T(8,128)S(1)}, f32[16,768]{1,0:T(8,128)S(1)}, u32[]{:S(2)}, u32[]{:S(2)}) %collective-permute-start.23) | collective-permute-done | bytes 49184 | tf_op jit(solution)/shard_map/ppermute | solution.py:270
  82.7 2.9 %collective-permute-start.24 = (f32[16,512]{1,0:T(8,128)S(1)}, f32[16,512]{1,0:T(8,128)S(1)}, u32[]{:S(2)}, u32[]{:S(2)}) collective-permute-start(f32[16,512]{1,0:T(8,128)S(1)} %get-tuple-element.38.a), channel_id=1, source_target_pairs={{0,4},{1,5},{2,6},{3,7},{4,0},{5,1},{6,2},{7,3},{8,12},{9,13},{10,... | collective-permute-start | bytes 98312 | tf_op jit(solution)/shard_map/ppermute | solution.py:270
  85.6 1.9 %collective-permute-done.24.b = f32[16,512]{1,0:T(8,128)S(1)} collective-permute-done((f32[16,512]{1,0:T(8,128)S(1)}, f32[16,512]{1,0:T(8,128)S(1)}, u32[]{:S(2)}, u32[]{:S(2)}) %collective-permute-start.24) | collective-permute-done | bytes 32800 | tf_op jit(solution)/shard_map/ppermute | solution.py:270
  88.6 2.4 %collective-permute-start.27 = (f32[16,768]{1,0:T(8,128)S(1)}, f32[16,768]{1,0:T(8,128)S(1)}, u32[]{:S(2)}, u32[]{:S(2)}) collective-permute-start(f32[16,768]{1,0:T(8,128)S(1)} %join.4.refs_0_), channel_id=1, source_target_pairs={{0,3},{1,2},{2,1},{3,0},{4,7},{5,6},{6,5},{7,4},{8,11},{9,10},{10,... | collective-permute-start | bytes 147464 | tf_op jit(solution)/shard_map/ppermute | solution.py:270
  95.0 2.9 %collective-permute-start.31 = (f32[16,512]{1,0:T(8,128)S(1)}, f32[16,512]{1,0:T(8,128)S(1)}, u32[]{:S(2)}, u32[]{:S(2)}) collective-permute-start(f32[16,512]{1,0:T(8,128)S(1)} %get-tuple-element.43.a), channel_id=1, source_target_pairs={{0,4},{1,5},{2,6},{3,7},{4,0},{5,1},{6,2},{7,3},{8,12},{9,13},{10,... | collective-permute-start | bytes 98312 | tf_op jit(solution)/shard_map/ppermute | solution.py:270
  98.0 1.9 %collective-permute-done.31.b = f32[16,512]{1,0:T(8,128)S(1)} collective-permute-done((f32[16,512]{1,0:T(8,128)S(1)}, f32[16,512]{1,0:T(8,128)S(1)}, u32[]{:S(2)}, u32[]{:S(2)}) %collective-permute-start.31) | collective-permute-done | bytes 32800 | tf_op jit(solution)/shard_map/ppermute | solution.py:270
  101.0 1.5 %collective-permute-start.29 = (f32[16,1536]{1,0:T(8,128)S(1)}, f32[16,1536]{1,0:T(8,128)S(1)}, u32[]{:S(2)}, u32[]{:S(2)}) collective-permute-start(f32[16,1536]{1,0:T(8,128)S(1)} %get-tuple-element.42.refs_0_), channel_id=1, source_target_pairs={{0,16},{8,24},{16,0},{24,8},{1,17},{9,25},{17,1},{25,9},{2,18},{10... | collective-permute-start | bytes 294920 | tf_op jit(solution)/shard_map/ppermute | solution.py:270
  102.8 1.9 %collective-permute-start.33 = (f32[16,768]{1,0:T(8,128)S(1)}, f32[16,768]{1,0:T(8,128)S(1)}, u32[]{:S(2)}, u32[]{:S(2)}) collective-permute-start(f32[16,768]{1,0:T(8,128)S(1)} %join.5.refs_0_), channel_id=1, source_target_pairs={{0,2},{1,3},{2,0},{3,1},{4,6},{5,7},{6,4},{7,5},{8,10},{9,11},{10,... | collective-permute-start | bytes 147464 | tf_op jit(solution)/shard_map/ppermute | solution.py:270
  104.7 1.7 %collective-permute-start.34 = (f32[16,768]{1,0:T(8,128)S(1)}, f32[16,768]{1,0:T(8,128)S(1)}, u32[]{:S(2)}, u32[]{:S(2)}) collective-permute-start(f32[16,768]{1,0:T(8,128)S(1)} %join.5.refs_0_), channel_id=1, source_target_pairs={{0,3},{1,2},{2,1},{3,0},{4,7},{5,6},{6,5},{7,4},{8,11},{9,10},{10,... | collective-permute-start | bytes 147464 | tf_op jit(solution)/shard_map/ppermute | solution.py:270
  106.9 2.8 %collective-permute-done.34.refs_3_ = f32[16,768]{1,0:T(8,128)S(1)} collective-permute-done((f32[16,768]{1,0:T(8,128)S(1)}, f32[16,768]{1,0:T(8,128)S(1)}, u32[]{:S(2)}, u32[]{:S(2)}) %collective-permute-start.34) | collective-permute-done | bytes 49184 | tf_op jit(solution)/shard_map/ppermute | solution.py:270
  109.9 1.7 %collective-permute-start.36 = (f32[16,768]{1,0:T(8,128)S(1)}, f32[16,768]{1,0:T(8,128)S(1)}, u32[]{:S(2)}, u32[]{:S(2)}) collective-permute-start(f32[16,768]{1,0:T(8,128)S(1)} %last.1.refs_4_), channel_id=1, source_target_pairs={{0,16},{8,24},{16,0},{24,8},{1,17},{9,25},{17,1},{25,9},{2,18},{10... | collective-permute-start | bytes 147464 | tf_op jit(solution)/shard_map/ppermute | solution.py:270
  111.7 2.3 %collective-permute-done.36.refs_6_ = f32[16,768]{1,0:T(8,128)S(1)} collective-permute-done((f32[16,768]{1,0:T(8,128)S(1)}, f32[16,768]{1,0:T(8,128)S(1)}, u32[]{:S(2)}, u32[]{:S(2)}) %collective-permute-start.36) | collective-permute-done | bytes 49184 | tf_op jit(solution)/shard_map/ppermute | solution.py:270
  (79 shorter events, 28.1 us)
Async XLA Ops:
  3.2 16.4 %collective-permute-start.9 = (f32[128,512]{1,0:T(8,128)}, f32[128,512]{1,0:T(8,128)S(1)}, u32[]{:S(2)}, u32[]{:S(2)}) collective-permute-start(f32[128,512]{1,0:T(8,128)} %get-tuple-element.31), channel_id=1, source_target_pairs={{0,4},{1,5},{2,6},{3,7},{4,0},{5,1},{6,2},{7,3},{8,12},{9,13},{10,... | collective-permute-start | bytes 786440 | tf_op jit(solution)/shard_map/ppermute | solution.py:270
  7.4 13.8 %collective-permute-start.6 = (f32[136,256]{1,0:T(8,128)}, f32[136,256]{1,0:T(8,128)S(1)}, u32[]{:S(2)}, u32[]{:S(2)}) collective-permute-start(f32[136,256]{1,0:T(8,128)} %get-tuple-element.30), channel_id=1, source_target_pairs={{0,1},{1,0},{2,3},{3,2},{4,5},{5,4},{6,7},{7,6},{8,9},{9,8},{10,11... | collective-permute-start | bytes 417800 | tf_op jit(solution)/shard_map/ppermute | solution.py:270
  8.9 12.3 %collective-permute-start.7 = (f32[136,256]{1,0:T(8,128)}, f32[136,256]{1,0:T(8,128)S(1)}, u32[]{:S(2)}, u32[]{:S(2)}) collective-permute-start(f32[136,256]{1,0:T(8,128)} %get-tuple-element.30), channel_id=1, source_target_pairs={{0,2},{1,3},{2,0},{3,1},{4,6},{5,7},{6,4},{7,5},{8,10},{9,11},{10,... | collective-permute-start | bytes 417800 | tf_op jit(solution)/shard_map/ppermute | solution.py:270
  10.5 11.1 %collective-permute-start.8 = (f32[136,256]{1,0:T(8,128)}, f32[136,256]{1,0:T(8,128)S(1)}, u32[]{:S(2)}, u32[]{:S(2)}) collective-permute-start(f32[136,256]{1,0:T(8,128)} %get-tuple-element.30), channel_id=1, source_target_pairs={{0,3},{1,2},{2,1},{3,0},{4,7},{5,6},{6,5},{7,4},{8,11},{9,10},{10,... | collective-permute-start | bytes 417800 | tf_op jit(solution)/shard_map/ppermute | solution.py:270
  19.6 9.2 %collective-permute-start.11 = (f32[128,512]{1,0:T(8,128)S(1)}, f32[128,512]{1,0:T(8,128)S(1)}, u32[]{:S(2)}, u32[]{:S(2)}) collective-permute-start(f32[128,512]{1,0:T(8,128)S(1)} %collective-permute-done.9.refs_0_), channel_id=1, source_target_pairs={{0,16},{8,24},{16,0},{24,8},{1,17},{9,25},{17,1},{25,9},{2,18},{10... | collective-permute-start | bytes 786440 | tf_op jit(solution)/shard_map/ppermute | solution.py:270
  21.6 13.8 %collective-permute-start.18 = (f32[128,768]{1,0:T(8,128)S(1)}, f32[128,768]{1,0:T(8,128)S(1)}, u32[]{:S(2)}, u32[]{:S(2)}) collective-permute-start(f32[128,768]{1,0:T(8,128)S(1)} %pack.1.refs_0_), channel_id=1, source_target_pairs={{0,16},{8,24},{16,0},{24,8},{1,17},{9,25},{17,1},{25,9},{2,18},{10... | collective-permute-start | bytes 1179656 | tf_op jit(solution)/shard_map/ppermute | solution.py:270
  23.2 24.4 %collective-permute-start.10 = (f32[128,512]{1,0:T(8,128)S(1)}, f32[128,512]{1,0:T(8,128)S(1)}, u32[]{:S(2)}, u32[]{:S(2)}) collective-permute-start(f32[128,512]{1,0:T(8,128)S(1)} %collective-permute-done.9.refs_0_), channel_id=1, source_target_pairs={{0,8},{8,0},{16,24},{24,16},{1,9},{9,1},{17,25},{25,17},{2,10},{10... | collective-permute-start | bytes 786440 | tf_op jit(solution)/shard_map/ppermute | solution.py:270
  28.8 20.6 %collective-permute-start.12 = (f32[128,512]{1,0:T(8,128)S(1)}, f32[128,512]{1,0:T(8,128)S(1)}, u32[]{:S(2)}, u32[]{:S(2)}) collective-permute-start(f32[128,512]{1,0:T(8,128)S(1)} %collective-permute-done.11.refs_2_), channel_id=1, source_target_pairs={{0,8},{8,0},{16,24},{24,16},{1,9},{9,1},{17,25},{25,17},{2,10},{10... | collective-permute-start | bytes 786440 | tf_op jit(solution)/shard_map/ppermute | solution.py:270
  28.8 36.0 %collective-permute-start.17 = (f32[128,768]{1,0:T(8,128)S(1)}, f32[128,768]{1,0:T(8,128)S(1)}, u32[]{:S(2)}, u32[]{:S(2)}) collective-permute-start(f32[128,768]{1,0:T(8,128)S(1)} %pack.1.refs_0_), channel_id=1, source_target_pairs={{0,8},{8,0},{16,24},{24,16},{1,9},{9,1},{17,25},{25,17},{2,10},{10... | collective-permute-start | bytes 1179656 | tf_op jit(solution)/shard_map/ppermute | solution.py:270
  35.5 29.3 %collective-permute-start.19 = (f32[128,768]{1,0:T(8,128)S(1)}, f32[128,768]{1,0:T(8,128)S(1)}, u32[]{:S(2)}, u32[]{:S(2)}) collective-permute-start(f32[128,768]{1,0:T(8,128)S(1)} %collective-permute-done.18.refs_2_), channel_id=1, source_target_pairs={{0,8},{8,0},{16,24},{24,16},{1,9},{9,1},{17,25},{25,17},{2,10},{10... | collective-permute-start | bytes 1179656 | tf_op jit(solution)/shard_map/ppermute | solution.py:270
  46.2 3.8 %collective-permute-start.3 = (f32[16,256]{1,0:T(8,128)S(1)}, f32[16,256]{1,0:T(8,128)S(1)}, u32[]{:S(2)}, u32[]{:S(2)}) collective-permute-start(f32[16,256]{1,0:T(8,128)S(1)} %first.1.refs_0_.refs_10_), channel_id=1, source_target_pairs={{0,1},{1,0},{2,3},{3,2},{4,5},{5,4},{6,7},{7,6},{8,9},{9,8},{10,11... | collective-permute-start | bytes 49160 | tf_op jit(solution)/shard_map/ppermute | solution.py:270
  49.4 4.6 %collective-permute-start.5 = (f32[16,256]{1,0:T(8,128)S(1)}, f32[16,256]{1,0:T(8,128)S(1)}, u32[]{:S(2)}, u32[]{:S(2)}) collective-permute-start(f32[16,256]{1,0:T(8,128)S(1)} %first.1.refs_0_.refs_10_), channel_id=1, source_target_pairs={{0,3},{1,2},{2,1},{3,0},{4,7},{5,6},{6,5},{7,4},{8,11},{9,10},{10,... | collective-permute-start | bytes 49160 | tf_op jit(solution)/shard_map/ppermute | solution.py:270
  56.0 5.2 %collective-permute-start.13 = (f32[16,512]{1,0:T(8,128)S(1)}, f32[16,512]{1,0:T(8,128)S(1)}, u32[]{:S(2)}, u32[]{:S(2)}) collective-permute-start(f32[16,512]{1,0:T(8,128)S(1)} %get-tuple-element.34), channel_id=1, source_target_pairs={{0,4},{1,5},{2,6},{3,7},{4,0},{5,1},{6,2},{7,3},{8,12},{9,13},{10,... | collective-permute-start | bytes 98312 | tf_op jit(solution)/shard_map/ppermute | solution.py:270
  61.2 3.9 %collective-permute-start.14 = (f32[16,512]{1,0:T(8,128)S(1)}, f32[16,512]{1,0:T(8,128)S(1)}, u32[]{:S(2)}, u32[]{:S(2)}) collective-permute-start(f32[16,512]{1,0:T(8,128)S(1)} %add.3.refs_0_), channel_id=1, source_target_pairs={{0,1},{1,0},{2,3},{3,2},{4,5},{5,4},{6,7},{7,6},{8,9},{9,8},{10,11... | collective-permute-start | bytes 98312 | tf_op jit(solution)/shard_map/ppermute | solution.py:270
  61.7 3.9 %collective-permute-start.15 = (f32[16,512]{1,0:T(8,128)S(1)}, f32[16,512]{1,0:T(8,128)S(1)}, u32[]{:S(2)}, u32[]{:S(2)}) collective-permute-start(f32[16,512]{1,0:T(8,128)S(1)} %add.3.refs_0_), channel_id=1, source_target_pairs={{0,2},{1,3},{2,0},{3,1},{4,6},{5,7},{6,4},{7,5},{8,10},{9,11},{10,... | collective-permute-start | bytes 98312 | tf_op jit(solution)/shard_map/ppermute | solution.py:270
  61.9 5.0 %collective-permute-start.16 = (f32[16,512]{1,0:T(8,128)S(1)}, f32[16,512]{1,0:T(8,128)S(1)}, u32[]{:S(2)}, u32[]{:S(2)}) collective-permute-start(f32[16,512]{1,0:T(8,128)S(1)} %add.3.refs_0_), channel_id=1, source_target_pairs={{0,3},{1,2},{2,1},{3,0},{4,7},{5,6},{6,5},{7,4},{8,11},{9,10},{10,... | collective-permute-start | bytes 98312 | tf_op jit(solution)/shard_map/ppermute | solution.py:270
  68.3 4.8 %collective-permute-start.20 = (f32[16,512]{1,0:T(8,128)S(1)}, f32[16,512]{1,0:T(8,128)S(1)}, u32[]{:S(2)}, u32[]{:S(2)}) collective-permute-start(f32[16,512]{1,0:T(8,128)S(1)} %get-tuple-element.36.a), channel_id=1, source_target_pairs={{0,4},{1,5},{2,6},{3,7},{4,0},{5,1},{6,2},{7,3},{8,12},{9,13},{10,... | collective-permute-start | bytes 98312 | tf_op jit(solution)/shard_map/ppermute | solution.py:270
  73.2 4.1 %collective-permute-start.21 = (f32[16,768]{1,0:T(8,128)S(1)}, f32[16,768]{1,0:T(8,128)S(1)}, u32[]{:S(2)}, u32[]{:S(2)}) collective-permute-start(f32[16,768]{1,0:T(8,128)S(1)} %join.3.refs_0_), channel_id=1, source_target_pairs={{0,1},{1,0},{2,3},{3,2},{4,5},{5,4},{6,7},{7,6},{8,9},{9,8},{10,11... | collective-permute-start | bytes 147464 | tf_op jit(solution)/shard_map/ppermute | solution.py:270
  74.3 4.1 %collective-permute-start.22 = (f32[16,768]{1,0:T(8,128)S(1)}, f32[16,768]{1,0:T(8,128)S(1)}, u32[]{:S(2)}, u32[]{:S(2)}) collective-permute-start(f32[16,768]{1,0:T(8,128)S(1)} %join.3.refs_0_), channel_id=1, source_target_pairs={{0,2},{1,3},{2,0},{3,1},{4,6},{5,7},{6,4},{7,5},{8,10},{9,11},{10,... | collective-permute-start | bytes 147464 | tf_op jit(solution)/shard_map/ppermute | solution.py:270
  76.3 5.0 %collective-permute-start.23 = (f32[16,768]{1,0:T(8,128)S(1)}, f32[16,768]{1,0:T(8,128)S(1)}, u32[]{:S(2)}, u32[]{:S(2)}) collective-permute-start(f32[16,768]{1,0:T(8,128)S(1)} %join.3.refs_0_), channel_id=1, source_target_pairs={{0,3},{1,2},{2,1},{3,0},{4,7},{5,6},{6,5},{7,4},{8,11},{9,10},{10,... | collective-permute-start | bytes 147464 | tf_op jit(solution)/shard_map/ppermute | solution.py:270
  82.7 4.8 %collective-permute-start.24 = (f32[16,512]{1,0:T(8,128)S(1)}, f32[16,512]{1,0:T(8,128)S(1)}, u32[]{:S(2)}, u32[]{:S(2)}) collective-permute-start(f32[16,512]{1,0:T(8,128)S(1)} %get-tuple-element.38.a), channel_id=1, source_target_pairs={{0,4},{1,5},{2,6},{3,7},{4,0},{5,1},{6,2},{7,3},{8,12},{9,13},{10,... | collective-permute-start | bytes 98312 | tf_op jit(solution)/shard_map/ppermute | solution.py:270
  87.5 4.1 %collective-permute-start.25 = (f32[16,768]{1,0:T(8,128)S(1)}, f32[16,768]{1,0:T(8,128)S(1)}, u32[]{:S(2)}, u32[]{:S(2)}) collective-permute-start(f32[16,768]{1,0:T(8,128)S(1)} %join.4.refs_0_), channel_id=1, source_target_pairs={{0,1},{1,0},{2,3},{3,2},{4,5},{5,4},{6,7},{7,6},{8,9},{9,8},{10,11... | collective-permute-start | bytes 147464 | tf_op jit(solution)/shard_map/ppermute | solution.py:270
  88.5 4.1 %collective-permute-start.26 = (f32[16,768]{1,0:T(8,128)S(1)}, f32[16,768]{1,0:T(8,128)S(1)}, u32[]{:S(2)}, u32[]{:S(2)}) collective-permute-start(f32[16,768]{1,0:T(8,128)S(1)} %join.4.refs_0_), channel_id=1, source_target_pairs={{0,2},{1,3},{2,0},{3,1},{4,6},{5,7},{6,4},{7,5},{8,10},{9,11},{10,... | collective-permute-start | bytes 147464 | tf_op jit(solution)/shard_map/ppermute | solution.py:270
  88.6 5.0 %collective-permute-start.27 = (f32[16,768]{1,0:T(8,128)S(1)}, f32[16,768]{1,0:T(8,128)S(1)}, u32[]{:S(2)}, u32[]{:S(2)}) collective-permute-start(f32[16,768]{1,0:T(8,128)S(1)} %join.4.refs_0_), channel_id=1, source_target_pairs={{0,3},{1,2},{2,1},{3,0},{4,7},{5,6},{6,5},{7,4},{8,11},{9,10},{10,... | collective-permute-start | bytes 147464 | tf_op jit(solution)/shard_map/ppermute | solution.py:270
  95.0 4.8 %collective-permute-start.31 = (f32[16,512]{1,0:T(8,128)S(1)}, f32[16,512]{1,0:T(8,128)S(1)}, u32[]{:S(2)}, u32[]{:S(2)}) collective-permute-start(f32[16,512]{1,0:T(8,128)S(1)} %get-tuple-element.43.a), channel_id=1, source_target_pairs={{0,4},{1,5},{2,6},{3,7},{4,0},{5,1},{6,2},{7,3},{8,12},{9,13},{10,... | collective-permute-start | bytes 98312 | tf_op jit(solution)/shard_map/ppermute | solution.py:270
  99.9 4.8 %collective-permute-start.32 = (f32[16,768]{1,0:T(8,128)S(1)}, f32[16,768]{1,0:T(8,128)S(1)}, u32[]{:S(2)}, u32[]{:S(2)}) collective-permute-start(f32[16,768]{1,0:T(8,128)S(1)} %join.5.refs_0_), channel_id=1, source_target_pairs={{0,1},{1,0},{2,3},{3,2},{4,5},{5,4},{6,7},{7,6},{8,9},{9,8},{10,11... | collective-permute-start | bytes 147464 | tf_op jit(solution)/shard_map/ppermute | solution.py:270
  101.0 8.7 %collective-permute-start.28 = (f32[16,1536]{1,0:T(8,128)S(1)}, f32[16,1536]{1,0:T(8,128)S(1)}, u32[]{:S(2)}, u32[]{:S(2)}) collective-permute-start(f32[16,1536]{1,0:T(8,128)S(1)} %get-tuple-element.42.refs_0_), channel_id=1, source_target_pairs={{0,8},{8,0},{16,24},{24,16},{1,9},{9,1},{17,25},{25,17},{2,10},{10... | collective-permute-start | bytes 294920 | tf_op jit(solution)/shard_map/ppermute | solution.py:270
  101.0 8.7 %collective-permute-start.29 = (f32[16,1536]{1,0:T(8,128)S(1)}, f32[16,1536]{1,0:T(8,128)S(1)}, u32[]{:S(2)}, u32[]{:S(2)}) collective-permute-start(f32[16,1536]{1,0:T(8,128)S(1)} %get-tuple-element.42.refs_0_), channel_id=1, source_target_pairs={{0,16},{8,24},{16,0},{24,8},{1,17},{9,25},{17,1},{25,9},{2,18},{10... | collective-permute-start | bytes 294920 | tf_op jit(solution)/shard_map/ppermute | solution.py:270
  102.5 7.2 %collective-permute-start.30 = (f32[16,1536]{1,0:T(8,128)S(1)}, f32[16,1536]{1,0:T(8,128)S(1)}, u32[]{:S(2)}, u32[]{:S(2)}) collective-permute-start(f32[16,1536]{1,0:T(8,128)S(1)} %get-tuple-element.42.refs_0_), channel_id=1, source_target_pairs={{0,24},{8,16},{16,8},{24,0},{1,25},{9,17},{17,9},{25,1},{2,26},{10... | collective-permute-start | bytes 294920 | tf_op jit(solution)/shard_map/ppermute | solution.py:270
  102.8 4.1 %collective-permute-start.33 = (f32[16,768]{1,0:T(8,128)S(1)}, f32[16,768]{1,0:T(8,128)S(1)}, u32[]{:S(2)}, u32[]{:S(2)}) collective-permute-start(f32[16,768]{1,0:T(8,128)S(1)} %join.5.refs_0_), channel_id=1, source_target_pairs={{0,2},{1,3},{2,0},{3,1},{4,6},{5,7},{6,4},{7,5},{8,10},{9,11},{10,... | collective-permute-start | bytes 147464 | tf_op jit(solution)/shard_map/ppermute | solution.py:270
  104.7 5.0 %collective-permute-start.34 = (f32[16,768]{1,0:T(8,128)S(1)}, f32[16,768]{1,0:T(8,128)S(1)}, u32[]{:S(2)}, u32[]{:S(2)}) collective-permute-start(f32[16,768]{1,0:T(8,128)S(1)} %join.5.refs_0_), channel_id=1, source_target_pairs={{0,3},{1,2},{2,1},{3,0},{4,7},{5,6},{6,5},{7,4},{8,11},{9,10},{10,... | collective-permute-start | bytes 147464 | tf_op jit(solution)/shard_map/ppermute | solution.py:270
  109.9 4.2 %collective-permute-start.36 = (f32[16,768]{1,0:T(8,128)S(1)}, f32[16,768]{1,0:T(8,128)S(1)}, u32[]{:S(2)}, u32[]{:S(2)}) collective-permute-start(f32[16,768]{1,0:T(8,128)S(1)} %last.1.refs_4_), channel_id=1, source_target_pairs={{0,16},{8,24},{16,0},{24,8},{1,17},{9,25},{17,1},{25,9},{2,18},{10... | collective-permute-start | bytes 147464 | tf_op jit(solution)/shard_map/ppermute | solution.py:270
  (15 other events, 249.4 us)
